TPU v7x, 32 devices: a whole 2x2x4 slice. The times are simulated.
32 devices in a mesh: groups: 2 (over x), tm: 8 (over z, y), band: 2 (over core).
Axes of the slice: x: 2, y: 2, z: 4, core: 2. Of those that a mesh axis runs over, the one named last changes fastest.
Arguments:
- series: float32 [262144], P(('groups', 'tm')), parts along dimension 0, may hold values from -40 to 40
- tail: float32 [512], P('groups'), parts along dimension 0, may hold values from -6 to 6
- band_starts: int32 [4], P('groups'), parts along dimension 0, may hold values from 0 to 3968, as said below
Outputs:
- row_profile: float32 [262144], P(('groups', 'tm')), parts along dimension 0
- col_profile: float32 [262144], P(('groups', 'tm')), parts along dimension 0
There are 2 independent parts, one for each index of `groups`. A program takes and returns all parts, laid end to end along the dimension named above; each array names one. Nothing has to cross between parts.
Inputs may be any that keep to these rules, and one draw needn't show every extreme that they name: `band_starts`: one entry equals 3968.
All inputs are finite; a program needn't handle non-finite values.
Results may differ from a plain program's by a relative error of at most 0.00061.
Values sent between devices are 32-bit elements; how exact they have to be, the bound alone decides.
No kernel may reach another device: no remote copies, remote signals or barrier semaphores. Data moves between devices by JAX's collectives and lax.ppermute only.
A program may use at most 64 MiB of HBM per device.

v0:
```python
import jax
import jax.numpy as jnp
from jax import lax
from jax.sharding import PartitionSpec as P

M = 256
TILE = 128
OFF_DEV = 128
BAND_SPAN = 4096
BAND_BLOCKS = 4


EPS = 1e-06
tile_batch = 16


def from_behind(block, axis, distance):
    devices = range(lax.axis_size(axis))
    route = [(i - distance, i) for i in devices if i - distance in devices]
    return lax.ppermute(block, axis, route)


def hankel(samples, tile_count):
    length = tile_count * TILE + M
    shifted = jnp.stack(
        [lax.slice_in_dim(samples, offset, offset + length) for offset in range(TILE)]
    )
    blocks = shifted.reshape(TILE, length // TILE, TILE)
    joined = jnp.concatenate(
        [blocks[:, stride : stride + tile_count] for stride in range(M // TILE)], axis=2
    )
    return jnp.swapaxes(joined, 0, 1)


def moments(matrix):
    center = jnp.mean(matrix, axis=-1)
    spread = matrix - center[..., None]
    factor = lax.rsqrt(jnp.sum(spread * spread, axis=-1) + M * EPS)
    return (center, factor)


def normed(matrix, center, factor):
    return ((matrix - center[..., None]) * factor[..., None]).astype(jnp.bfloat16)


def score_group(row_z, col_z, room_left):
    tile_count = row_z.shape[0]
    near_scores = jnp.einsum("tim,tjm->tij", row_z, col_z[:-1], preferred_element_type=jnp.float32)
    far_scores = jnp.einsum(
        "tim,tjm->tij", row_z, col_z[1:, :OFF_DEV], preferred_element_type=jnp.float32
    )
    row_near = lax.broadcasted_iota(jnp.int32, (TILE, TILE), 0)
    col_near = lax.broadcasted_iota(jnp.int32, (TILE, TILE), 1)
    row_far = lax.broadcasted_iota(jnp.int32, (TILE, OFF_DEV), 0)
    col_far = lax.broadcasted_iota(jnp.int32, (TILE, OFF_DEV), 1)
    tile_index = jnp.arange(tile_count, dtype=jnp.int32)[:, None, None]
    keep_near = (
        (col_near >= row_near)[None]
        & (col_near - row_near < OFF_DEV)[None]
        & (tile_index * TILE + col_near[None] < room_left)
    )
    keep_far = (TILE + col_far - row_far < OFF_DEV)[None] & (
        (tile_index + 1) * TILE + col_far[None] < room_left
    )
    near_scores = jnp.where(keep_near, near_scores, -1.0)
    far_scores = jnp.where(keep_far, far_scores, -1.0)
    best_rows = jnp.maximum(near_scores.max(axis=2), far_scores.max(axis=2)).reshape(-1)
    floor_row = jnp.full((1, TILE), -1.0, jnp.float32)
    upper_part = jnp.concatenate([near_scores.max(axis=1), floor_row], axis=0)
    far_cols = far_scores.max(axis=1)
    lower_part = jnp.concatenate([floor_row, far_cols], axis=0)
    return (best_rows, jnp.maximum(upper_part, lower_part).reshape(-1))


def place_columns(col_groups, start, buffer_len):
    group_rows = tile_batch * TILE
    count = col_groups.shape[0]
    main_part = col_groups[:, :group_rows].reshape(-1)
    carry_part = jnp.concatenate(
        [col_groups[:, group_rows:], jnp.full((count, group_rows - TILE), -1.0, jnp.float32)],
        axis=1,
    ).reshape(-1)
    shifted = jnp.concatenate([jnp.full((group_rows,), -1.0, jnp.float32), carry_part])[
        : count * group_rows + TILE
    ]
    reached = jnp.maximum(
        jnp.concatenate([main_part, jnp.full((TILE,), -1.0, jnp.float32)]), shifted
    )
    buffer_all = jnp.full((buffer_len,), -1.0, jnp.float32)
    return lax.dynamic_update_slice(buffer_all, reached, (start,))


def body(series, tail, band_starts):
    block_len = series.shape[0]
    group_rows = tile_batch * TILE
    group_count = block_len // group_rows
    position = lax.axis_index("tm")
    devices = lax.axis_size("tm")
    distance = BAND_BLOCKS
    following = from_behind(series[:M], "tm", -1)
    following = jnp.where(position == devices - 1, tail, following)
    extended = jnp.concatenate([series, following])
    row_source = jnp.concatenate([extended, jnp.zeros((TILE,), jnp.float32)])

    def own_group(group_index):
        row_piece = lax.dynamic_slice_in_dim(
            row_source, group_index * group_rows, group_rows + M + TILE
        )
        matrix = hankel(row_piece, tile_batch)
        center, factor = moments(matrix)
        return (center.reshape(-1), factor.reshape(-1), normed(matrix, center, factor))

    centers, factors, row_z = lax.map(own_group, jnp.arange(group_count, dtype=jnp.int32))
    centers = centers.reshape(block_len)
    factors = factors.reshape(block_len)
    padding = jnp.zeros((2 * TILE,), jnp.float32)
    far_samples = from_behind(extended, "tm", -distance)
    next_samples = from_behind(series[M : M + BAND_SPAN], "tm", -distance - 1)
    pair_samples = jnp.concatenate([far_samples, next_samples, padding])
    buffer_len = block_len + BAND_SPAN + TILE
    band_count = band_starts.shape[0]
    band_here = lax.axis_index("band")
    offset_start = jnp.sum(
        jnp.where(jnp.arange(band_count, dtype=jnp.int32) == band_here, band_starts, 0)
    )
    room_all = (devices - position - distance) * block_len - offset_start

    def pair_group(inputs):
        group_index, group_z = inputs
        col_begin = offset_start + group_index * group_rows
        col_piece = lax.dynamic_slice_in_dim(pair_samples, col_begin, (tile_batch + 2) * TILE + M)
        matrix = hankel(col_piece, tile_batch + 1)
        center, factor = moments(matrix)
        col_z = normed(matrix, center, factor)
        return score_group(group_z, col_z, room_all - group_index * group_rows)

    row_best, col_groups = lax.map(pair_group, (jnp.arange(group_count, dtype=jnp.int32), row_z))
    lifted = place_columns(col_groups, offset_start, buffer_len) + 1.0
    returned = from_behind(lifted[:block_len], "tm", distance)
    returned_head = from_behind(lifted[block_len : block_len + BAND_SPAN], "tm", distance + 1)
    col_best = (
        jnp.maximum(
            returned,
            jnp.concatenate([returned_head, jnp.zeros((block_len - BAND_SPAN,), jnp.float32)]),
        )
        - 1.0
    )
    return lax.pmax((row_best.reshape(block_len), col_best), "band")


def solution(mesh):
    placed = (P(("groups", "tm")), P("groups"), P("groups"))
    return jax.shard_map(
        body,
        mesh=mesh,
        in_specs=placed,
        out_specs=(P(("groups", "tm")), P(("groups", "tm"))),
        check_vma=False,
    )
```

profile of v0, /device:TPU:13, one launch (start us, length us, event | category | flops | bytes accessed | tf_op | source)
XLA Modules:
  0.0 257.1 jit_solution(17641519265853953807)
XLA Ops:
  7.9 2.1 collective-permute-start
  18.3 81.0 %while.22 = (s32[]{:T(128)}, bf16[8,16,128,256]{3,2,1,0:T(8,128)(2,1)}, s32[8]{0:T(128)S(1)}, f32[16768]{0:T(1024)S(1)}, s32[]{:T(128)}, /*index=5*/s32[1]{0:T(1...) while((s32[]{:T(128)}, ...), condition=%wide.region_3.4_spmd, body=%wide.region_0.3_spmd.sunk | while | flops 5243013 | bytes 18689660 | solution.py:113
  23.8 1.9 stack.1160
  33.9 1.9 stack.1160
  44.0 1.9 stack.1160
  54.1 1.9 stack.1160
  64.2 1.9 stack.1160
  74.4 1.9 stack.1160
  84.5 1.9 stack.1160
  94.6 1.9 stack.1160
  99.4 114.6 %while.23 = (s32[]{:T(128)}, f32[8,2048]{1,0:T(8,128)S(1)}, f32[8,2176]{1,0:T(8,128)S(1)}, s32[8]{0:T(128)S(1)}, s32[]{:T(128)}, /*index=5*/bf16[8,16,128,256]{3...) while((s32[]{:T(128)}, f32[8,2048]{1,0:T(8,128)S(1)}, ...), condition=%wide.region_12.13_spmd, body=%wide.region_5.12_spmd.sunk | while | flops 277246400 | bytes 24204612 | solution.py:137
  105.6 2.0 stack.1289
  109.8 1.8 fusion.80
  119.9 2.0 stack.1289
  124.1 1.8 fusion.80
  125.9 1.8 fusion.79
  134.3 2.0 stack.1289
  138.5 1.8 fusion.80
  140.2 1.8 fusion.79
  148.6 2.0 stack.1289
  154.6 1.8 fusion.79
  162.9 2.0 stack.1289
  167.1 1.8 fusion.80
  168.9 1.8 fusion.79
  177.2 2.0 stack.1289
  183.2 1.8 fusion.79
  191.5 2.0 stack.1289
  195.7 1.8 fusion.80
  197.5 1.8 fusion.79
  205.8 2.0 stack.1289
  214.5 7.0 %collective-permute-start.3 = (f32[16384]{0:T(1024)S(1)}, f32[16384]{0:T(1024)S(1)}, u32[]{:S(2)}, u32[]{:S(2)}) collective-permute-start(f32[16384]{0:T(1024)S(1)} %slice.820), channel_id=1, source_target_pairs={{0,8},{2,10},{4,12},{6,14},{1,9},{3,11},{5,13},{7,15},{16,24},{18,... | collective-permute-start | bytes 196616 | tf_op jit(solution)/shard_map/ppermute | solution.py:20
  223.7 23.7 %all-reduce.9.cloned.1.call-done = (f32[16384]{0:T(1024)}, f32[16384]{0:T(1024)}) async-done(((f32[16384]{0:T(1024)}, f32[16384]{0:T(1024)}), (f32[16384]{0:T(1024)}, f32[16384]{0:T(1024)})) %all-reduce.9.cloned.1.call-update) | async-done | bytes 131088 | tf_op jit(solution)/shard_map/pmax | solution.py:148
  (2427 shorter events, 130.7 us)
Async XLA Ops:
  7.2 240.2 %all-reduce.9.cloned.1.call-start = ((), (), s32[]{:S(2)}) async-start(), calls=%async_computation | async-start | bytes 262144 | tf_op jit(solution)/shard_map/pmax | solution.py:148
  7.9 7.4 %collective-permute-start = (f32[256]{0:T(256)S(1)}, f32[256]{0:T(256)S(1)}, u32[]{:S(2)}, u32[]{:S(2)}) collective-permute-start(f32[256]{0:T(256)S(1)} %slice.807), channel_id=1, source_target_pairs={{2,0},{4,2},{6,4},{8,6},{10,8},{12,10},{14,12},{3,1},{5,3},{7,5},{... | collective-permute-start | bytes 3080 | tf_op jit(solution)/shard_map/ppermute | solution.py:20
  10.8 88.6 %collective-permute-start.2 = (f32[4096]{0:T(1024)S(1)}, f32[4096]{0:T(1024)S(1)}, u32[]{:S(2)}, u32[]{:S(2)}) collective-permute-start(f32[4096]{0:T(1024)S(1)} %slice.808), channel_id=1, source_target_pairs={{10,0},{12,2},{14,4},{11,1},{13,3},{15,5},{26,16},{28,18},{30,20},... | collective-permute-start | bytes 49160 | tf_op jit(solution)/shard_map/ppermute | solution.py:20
  17.0 82.3 %collective-permute-start.1 = (f32[16640]{0:T(1024)S(1)}, f32[16640]{0:T(1024)S(1)}, u32[]{:S(2)}, u32[]{:S(2)}) collective-permute-start(f32[16640]{0:T(1024)S(1)} %pad_maximum_fusion.2), channel_id=1, source_target_pairs={{8,0},{10,2},{12,4},{14,6},{9,1},{11,3},{13,5},{15,7},{24,16},{26,... | collective-permute-start | bytes 199688 | tf_op jit(solution)/shard_map/ppermute | solution.py:20
  214.5 8.5 %collective-permute-start.3 = (f32[16384]{0:T(1024)S(1)}, f32[16384]{0:T(1024)S(1)}, u32[]{:S(2)}, u32[]{:S(2)}) collective-permute-start(f32[16384]{0:T(1024)S(1)} %slice.820), channel_id=1, source_target_pairs={{0,8},{2,10},{4,12},{6,14},{1,9},{3,11},{5,13},{7,15},{16,24},{18,... | collective-permute-start | bytes 196616 | tf_op jit(solution)/shard_map/ppermute | solution.py:20
  221.5 1.3 collective-permute-start.4
Sparse Core Ops, SparseCore 0:
  223.8 23.4 all-reduce.8
where the time goes:
time: 259 us; the launch traced here: 257 us
  local copies, waits for them, and re-layouts  111 us (43%)
  other arithmetic  39.6 us (15%)
  matrix products  28 us (11%)
  loops' own time  26.3 us (10%)
  waiting for transfers between devices  23.8 us (9%)
  between operations  16.8 us (6%)
  starting transfers between devices  11.8 us (5%)
    another operation x2064, local copies, waits for them, and re-layouts, hankel(): jnp.stack([lax.slice_in_dim(samples, offset, offset + length) for offset...  60.5 us
    slice x144, local copies, waits for them, and re-layouts, hankel(): lax.slice_in_dim(samples, offset, offset + length)  28.4 us
    pmax x1, waiting for transfers between devices, body(): return lax.pmax((row_best.reshape(block_len), col_best), 'band')  23.7 us
    another operation x1, loops' own time, body(): lax.map(pair_group, (jnp.arange(group_count, dtype=jnp.int32), row_z))  16.2 us
    dot_general x8, matrix products, score_group(): jnp.einsum('tim,tjm->tij', row_z, col_z[:-1], preferred_element_type=jnp....  14 us
    dot_general x8, matrix products, score_group(): jnp.einsum('tim,tjm->tij', row_z, col_z[1:, :OFF_DEV], preferred_element_...  14 us
    dynamic_update_slice x8, other arithmetic, body(): lax.map(own_group, jnp.arange(group_count, dtype=jnp.int32))  12.2 us
    ppermute x5, starting transfers between devices, from_behind(): return lax.ppermute(block, axis, route)  11.7 us
  transfers between devices with their start and end apart: 6, of which 2 were waited for; matrix products, arithmetic and copies ran while one was open for 29% of the time, Pallas kernels for 0%

commit v1 on v0

v1 whole, which is shorter than its diff:
```python
import functools

import jax
import jax.numpy as jnp
from jax import lax
from jax.experimental import pallas as pl
from jax.experimental.pallas import tpu as pltpu
from jax.sharding import PartitionSpec as P

M = 256
LANES = 128
OFF_DEV = 128
BAND_SPAN = 4096
BAND_BASE = 65536
EPS = 1e-06

WIN = M // LANES
BEFORE = BAND_SPAN // LANES + 1
AFTER = BEFORE + WIN


def window_moments(samples):
    count = samples.shape[0]
    lane = lax.broadcasted_iota(jnp.int32, samples.shape, 1)

    def ahead(values, distance):
        below = pltpu.roll(values, count - 1, 0)
        if distance == LANES:
            return below
        joined = jnp.where(lane < distance, below, values)
        return pltpu.roll(joined, LANES - distance, 1)

    center = samples
    spread = None
    size = 1
    while size < M:
        later = ahead(center, size)
        gap = later - center
        step = gap * gap * (0.5 * size)
        spread = step if spread is None else spread + ahead(spread, size) + step
        center = 0.5 * (later + center)
        size *= 2
    return center, spread


def profile_kernel(
    geometry,
    starts_ref,
    own_ref,
    halo_ref,
    tail_ref,
    main_ref,
    side_ref,
    last_ref,
    out_ref,
    own_s,
    pair_s,
    shifted,
    center_s,
    factor_s,
    near_s,
):
    devices, distance, rows, tiles, role = geometry
    bands = starts_ref.shape[0]
    position = lax.axis_index("tm")
    first_row = lax.axis_index("band") * tiles if tiles < rows else 0
    is_col = position >= distance if role is None else role
    block = rows * LANES

    own_s[pl.ds(0, rows), :] = own_ref[...]
    own_s[pl.ds(rows, WIN), :] = jnp.where(position == devices - 1, tail_ref[...], halo_ref[...])
    pair_s[pl.ds(rows + AFTER, pair_s.shape[0] - rows - AFTER), :] = jnp.zeros(
        (pair_s.shape[0] - rows - AFTER, LANES), jnp.float32
    )

    @pl.when(jnp.logical_not(is_col))
    def _():
        pair_s[pl.ds(0, rows), :] = main_ref[...]
        pair_s[pl.ds(rows, AFTER), :] = side_ref[...]

        @pl.when(position == devices - distance - 1)
        def _():
            pair_s[pl.ds(rows, WIN), :] = tail_ref[...]

    @pl.when(is_col)
    def _():
        pair_s[pl.ds(0, BEFORE), :] = side_ref[pl.ds(WIN, BEFORE), :]
        pair_s[pl.ds(BEFORE, rows), :] = main_ref[...]
        pair_s[pl.ds(BEFORE + rows, WIN), :] = last_ref[...]

    lane = lax.broadcasted_iota(jnp.int32, (1, LANES), 1)
    reach = tiles + 1 + WIN
    begins = []
    for band in range(bands):
        start = starts_ref[band]
        begin = jnp.where(is_col, BEFORE * LANES - (OFF_DEV - 1) - start, start) + first_row * LANES
        begins.append(begin)
        whole, part = begin // LANES, begin % LANES
        piece = pair_s[pl.ds(whole, reach + 1), :]
        turned = pltpu.roll(piece, LANES - part, 1)
        shifted[band, pl.ds(0, reach), :] = jnp.where(lane < LANES - part, turned[:-1], turned[1:])
    shifted[bands, pl.ds(0, reach - 1), :] = own_s[pl.ds(first_row, reach - 1), :]
    center, spread = window_moments(shifted[...].reshape(-1, LANES))
    center_s[...] = center.reshape(center_s.shape)
    factor_s[...] = lax.rsqrt(spread + M * EPS).reshape(factor_s.shape)

    row_id = lax.broadcasted_iota(jnp.int32, (LANES, LANES), 0)
    col_id = lax.broadcasted_iota(jnp.int32, (LANES, LANES), 1)
    source = (row_id + col_id) % LANES
    straight = row_id + col_id < LANES
    upper = row_id >= col_id

    def turned_row(stream, row):
        line = jnp.broadcast_to(shifted[stream, pl.ds(row, 1), :], (LANES, LANES))
        return jnp.take_along_axis(line, source, axis=1)

    def hankel(stream, row):
        a, b, c = (turned_row(stream, row + s) for s in range(WIN + 1))
        return jnp.where(straight, a, b), jnp.where(straight, b, c)

    def column_form(values, tile):
        line = jnp.broadcast_to(values[pl.ds(tile, 1), :], (LANES, LANES))
        return jnp.transpose(line)

    def own_z(tile):
        low, high = hankel(bands, tile)
        center = center_s[bands, pl.ds(tile, 1), :]
        factor = factor_s[bands, pl.ds(tile, 1), :]
        return jnp.concatenate(
            [((low - center) * factor).astype(jnp.bfloat16), ((high - center) * factor).astype(jnp.bfloat16)],
            axis=0,
        )

    def pair_z(band, tile):
        low, high = hankel(band, tile)
        center = column_form(center_s.at[band], tile)
        factor = column_form(factor_s.at[band], tile)
        return jnp.concatenate(
            [((low - center) * factor).astype(jnp.bfloat16), ((high - center) * factor).astype(jnp.bfloat16)],
            axis=1,
        )

    low_edge = BEFORE * LANES - (position - distance) * block
    high_edge = (devices - position - distance) * block
    lo = jnp.where(is_col, low_edge, 0)
    hi = jnp.where(is_col, 1 << 30, high_edge)

    def step(masked, tile, before):
        here = own_z(jnp.minimum(tile, tiles - 1))
        both = jnp.concatenate([before, here], axis=1)
        far = near = None
        for band in range(bands):
            z = pair_z(band, tile)
            scores = jnp.dot(z, both, preferred_element_type=jnp.float32)
            if masked:
                index = begins[band] + tile * LANES + lax.broadcasted_iota(jnp.int32, (LANES, 1), 0)
                scores = jnp.where((index >= lo) & (index < hi), scores, -1.0)
            far = scores[:, :LANES] if far is None else jnp.maximum(far, scores[:, :LANES])
            near = scores[:, LANES:] if near is None else jnp.maximum(near, scores[:, LANES:])
        best = jnp.where(upper, near_s[...], far)
        best = jnp.maximum(jnp.max(best, axis=0, keepdims=True), -1.0)
        near_s[...] = near

        @pl.when(tile > 0)
        def _():
            out_ref[pl.ds(tile - 1, 1), :] = best

        return here

    first_full, last_full = jnp.int32(0), jnp.int32(tiles + 1)
    for begin in begins:
        first_full = jnp.maximum(first_full, (lo - begin + LANES - 1) // LANES)
        last_full = jnp.minimum(last_full, (hi - begin) // LANES)
    first_full = jnp.clip(first_full, 0, tiles + 1)
    last_full = jnp.clip(last_full, first_full, tiles + 1)
    before = jnp.zeros((M, LANES), jnp.bfloat16)
    before = lax.fori_loop(0, first_full, functools.partial(step, True), before)
    before = lax.fori_loop(first_full, last_full, functools.partial(step, False), before)
    lax.fori_loop(last_full, tiles + 1, functools.partial(step, True), before)


def profile(geometry, starts, own, halo, tail, main, side, last):
    devices, distance, rows, tiles, role = geometry
    bands = starts.shape[0]
    vmem = pl.BlockSpec(memory_space=pltpu.VMEM)
    pad = -(-(tiles + 2 + WIN) // 8) * 8
    return pl.pallas_call(
        functools.partial(profile_kernel, geometry),
        out_shape=jax.ShapeDtypeStruct((tiles, LANES), jnp.float32),
        in_specs=[pl.BlockSpec(memory_space=pltpu.SMEM)] + [vmem] * 6,
        out_specs=vmem,
        scratch_shapes=[
            pltpu.VMEM((rows + 8, LANES), jnp.float32),
            pltpu.VMEM((-(-(rows + AFTER + 2) // 8) * 8, LANES), jnp.float32),
            pltpu.VMEM((bands + 1, pad, LANES), jnp.float32),
            pltpu.VMEM((bands + 1, pad, LANES), jnp.float32),
            pltpu.VMEM((bands + 1, pad, LANES), jnp.float32),
            pltpu.VMEM((LANES, LANES), jnp.float32),
        ],
    )(starts, own, halo, tail, main, side, last)


def body(split, series, tail, band_starts):
    block_len = series.shape[0]
    rows = block_len // LANES
    devices = lax.axis_size("tm")
    distance = BAND_BASE // block_len
    cores = lax.axis_size("band") if split else 1
    tiles = rows // cores
    position = lax.axis_index("tm")
    own = series.reshape(rows, LANES)
    tail = tail.reshape(WIN, LANES)
    head = own[:WIN]

    def move(value, steps):
        route = [(d - s, d) for d, s in steps if 0 <= d - s < devices]
        return lax.ppermute(value, "tm", route)

    everyone = range(devices)
    halo = move(head, [(d, -1) for d in everyone])
    row_side = [d for d in everyone if d < devices - distance]
    col_side = [d for d in everyone if d >= distance]
    last = move(head, [(d, distance - 1) for d in col_side])
    if devices <= 2 * distance:
        main = move(own, [(d, -distance) for d in row_side] + [(d, distance) for d in col_side])
        begin = jnp.where(position >= distance, 0, rows - AFTER)
        piece = lax.dynamic_slice_in_dim(own, begin, AFTER)
        side = move(piece, [(d, -distance - 1) for d in row_side] + [(d, distance + 1) for d in col_side])
        found = [profile((devices, distance, rows, tiles, None), band_starts, own, halo, tail, main, side, last)]
    else:
        main = move(own, [(d, -distance) for d in row_side])
        side = move(own[:AFTER], [(d, -distance - 1) for d in row_side])
        found = [profile((devices, distance, rows, tiles, False), band_starts, own, halo, tail, main, side, last)]
        main = move(own, [(d, distance) for d in col_side])
        side = move(own[rows - AFTER :], [(d, distance + 1) for d in col_side])
        found.append(
            profile((devices, distance, rows, tiles, True), band_starts, own, halo, tail, main, side, last)
        )
    if cores > 1:
        ring = [(i, (i + 1) % cores) for i in range(cores)]
        first = lax.axis_index("band") == 0
        whole = []
        for part in found:
            other = lax.ppermute(part, "band", ring)
            whole.append(jnp.concatenate([jnp.where(first, part, other), jnp.where(first, other, part)]))
        found = whole
    is_row, is_col = position < devices - distance, position >= distance
    row_best = jnp.where(is_row, found[0], -1.0)
    col_best = jnp.where(is_col, found[-1], -1.0)
    return row_best.reshape(-1), col_best.reshape(-1)


SPLIT = True


def solution(mesh):
    placed = (P(("groups", "tm")), P("groups"), P("groups"))
    split = SPLIT and mesh.shape["band"] == 2
    return jax.shard_map(
        functools.partial(body, split),
        mesh=mesh,
        in_specs=placed,
        out_specs=(P(("groups", "tm")), P(("groups", "tm"))),
        check_vma=False,
    )
```

time: 259 us -> 68.5 us (0.26)
  local copies, waits for them, and re-layouts: 111 us -> 2.08 us
  Pallas kernels: 0 us -> 45.7 us
  other arithmetic: 39.6 us -> 1.43 us
  matrix products: 28 us -> 0 us
  loops' own time: 26.3 us -> 0 us
  waiting for transfers between devices: 23.8 us -> 4.35 us
  between operations: 16.8 us -> 0.7 us
    another operation x2064 -> x0, local copies, waits for them, and re-layouts: 60.5 us -> none  [hankel(): jnp.stack([lax.slice_in_dim(samples, offset, offset + length) for offset...]
    pallas_call x0 -> x1, Pallas kernels: none -> 45.7 us  [profile(): pl.pallas_call(functools.partial(profile_kernel, geometry), out_shape=jax...]
    slice x165 -> x1, local copies, waits for them, and re-layouts: 33.8 us -> 0.69 us  [body(): head = own[:WIN]]
    dot_general x16 -> x0, matrix products: 28 us -> none  [the longest x8 14 us: score_group(): jnp.einsum('tim,tjm->tij', row_z, col_z[:-1], preferred_element_type=jnp....]
    another operation x2 -> x0, loops' own time: 26.3 us -> none  [the longest x1 16.2 us: body(): lax.map(pair_group, (jnp.arange(group_count, dtype=jnp.int32), row_z))]
    pmax x1 -> x0, waiting for transfers between devices: 23.7 us -> none  [body(): return lax.pmax((row_best.reshape(block_len), col_best), 'band')]
    reduce_sum x33 -> x0, other arithmetic: 17.7 us -> none  [the longest x16 10.6 us: moments(): factor = lax.rsqrt(jnp.sum(spread * spread, axis=-1) + M * EPS)]
    dynamic_update_slice x9 -> x0, other arithmetic: 12.5 us -> none  [the longest x8 12.2 us: body(): lax.map(own_group, jnp.arange(group_count, dtype=jnp.int32))]
  transfers between devices with their start and end apart: 6 -> 5, of which waited for: 2 -> 2; matrix products, arithmetic and copies ran while one was open for 29% -> 2% of each run, Pallas kernels for 0% -> 0%
where the time goes in v1:
time: 68.5 us; the launch traced here: 68.1 us
  Pallas kernels  45.7 us (67%)
  starting transfers between devices  13.9 us (20%)
  waiting for transfers between devices  4.35 us (6%)
  local copies, waits for them, and re-layouts  2.08 us (3%)
  other arithmetic  1.43 us (2%)
  between operations  0.7 us (1%)
    pallas_call x1, Pallas kernels, profile(): pl.pallas_call(functools.partial(profile_kernel, geometry), out_shape=jax...  45.7 us
    ppermute x4, starting transfers between devices, move(): return lax.ppermute(value, 'tm', route)  11.2 us
    ppermute x4, waiting for transfers between devices, move(): return lax.ppermute(value, 'tm', route)  3.28 us
    ppermute x1, starting transfers between devices, body(): other = lax.ppermute(part, 'band', ring)  2.66 us
  transfers between devices with their start and end apart: 5, of which 2 were waited for; matrix products, arithmetic and copies ran while one was open for 2% of the time, Pallas kernels for 0%

profile of v1, /device:TPU:13, one launch (start us, length us, event | category | flops | bytes accessed | tf_op | source)
XLA Modules:
  0.0 68.1 jit_solution(11966195802962299367)
XLA Ops:
  0.6 2.4 %collective-permute-start.1 = (f32[128,128]{1,0:T(8,128)}, f32[128,128]{1,0:T(8,128)S(1)}, u32[]{:S(2)}, u32[]{:S(2)}) collective-permute-start(f32[128,128]{1,0:T(8,128)} %bitcast.8), channel_id=1, source_target_pairs={{8,0},{10,2},{12,4},{14,6},{0,8},{2,10},{4,12},{6,14},{9,1},{11,3}... | collective-permute-start | bytes 196616 | tf_op jit(solution)/shard_map/ppermute | solution.py:217
  3.0 0.8 %constant_dynamic-slice_fusion = f32[35,128]{1,0:T(8,128)S(1)} fusion(f32[128,128]{1,0:T(8,128)} %bitcast.9, s32[]{:T(128)S(6)} %select_n.41), kind=kLoop, calls=%fused_computation.6 | loop fusion | bytes 35844 | tf_op jit(solution)/shard_map/dynamic_slice | solution.py:227
  3.8 0.7 collective-permute-start.2
  4.4 0.7 %slice_bitcast_fusion = f32[2,128]{1,0:T(2,128)S(1)} fusion(f32[16384]{0:T(1024)} %param.3), kind=kLoop, calls=%fused_computation.5 | loop fusion | bytes 2048 | tf_op jit(solution)/shard_map/slice | solution.py:213
  5.1 6.3 %collective-permute-start.3 = (f32[2,128]{1,0:T(2,128)S(1)}, f32[2,128]{1,0:T(2,128)S(1)}, u32[]{:S(2)}, u32[]{:S(2)}) collective-permute-start(f32[2,128]{1,0:T(2,128)S(1)} %slice_bitcast_fusion), channel_id=1, source_target_pairs={{2,8},{4,10},{6,12},{8,14},{3,9},{5,11},{7,13},{9,15},{18,24},{20,... | collective-permute-start | bytes 3080 | tf_op jit(solution)/shard_map/ppermute | solution.py:217
  11.4 1.9 %collective-permute-start = (f32[2,128]{1,0:T(2,128)S(1)}, f32[2,128]{1,0:T(2,128)S(1)}, u32[]{:S(2)}, u32[]{:S(2)}) collective-permute-start(f32[2,128]{1,0:T(2,128)S(1)} %slice_bitcast_fusion), channel_id=1, source_target_pairs={{2,0},{4,2},{6,4},{8,6},{10,8},{12,10},{14,12},{3,1},{5,3},{7,5},{... | collective-permute-start | bytes 3080 | tf_op jit(solution)/shard_map/ppermute | solution.py:217
  13.3 0.0 collective-permute-done.3.last_ref
  13.4 0.0 copy-start.2
  13.4 3.3 %collective-permute-done.halo_ref = f32[2,128]{1,0:T(2,128)S(1)} collective-permute-done((f32[2,128]{1,0:T(2,128)S(1)}, f32[2,128]{1,0:T(2,128)S(1)}, u32[]{:S(2)}, u32[]{:S(2)}) %collective-permute-start) | collective-permute-done | bytes 1056 | tf_op jit(solution)/shard_map/ppermute | solution.py:217
  16.6 0.0 copy-start.3
  16.6 0.0 collective-permute-done.2.side_ref
  16.6 0.0 copy-start.1
  16.6 0.0 collective-permute-done.1.main_ref
  16.6 0.0 copy-start
  16.7 0.0 copy-done.2
  16.7 0.5 copy-done.3
  17.2 0.1 copy-done.1
  17.2 0.0 copy-done
  17.3 45.7 %shard_map.50 = f32[64,128]{1,0:T(8,128)} custom-call(s32[2]{0:T(128)} %starts_ref.1, f32[128,128]{1,0:T(8,128)} %bitcast.10, f32[2,128]{1,0:T(2,128)} %copy-done.3, f32[2,128]{1,0:T(2,128)} %bitcast.11, f32[128,128]{1,0:T(8,128)} %copy-done, f32[35,128]{1,0:T(8,128)} %copy-done.1, f32[2,128]{1,0:T(2,128)} %copy-done.2), custom_call_target="tpu_custom_call" | custom-call | tf_op jit(solution)/shard_map/pallas_call | solution.py:187
  62.9 2.7 %collective-permute-start.4 = (f32[64,128]{1,0:T(8,128)}, f32[64,128]{1,0:T(8,128)S(1)}, u32[]{:S(2)}, u32[]{:S(2)}) collective-permute-start(f32[64,128]{1,0:T(8,128)} %shard_map.50), channel_id=1, source_target_pairs={{0,1},{1,0},{2,3},{3,2},{4,5},{5,4},{6,7},{7,6},{8,9},{9,8},{10,11... | collective-permute-start | bytes 98312 | tf_op jit(solution)/shard_map/ppermute | solution.py:244
  65.6 1.1 %collective-permute-done.4 = f32[64,128]{1,0:T(8,128)S(1)} collective-permute-done((f32[64,128]{1,0:T(8,128)}, f32[64,128]{1,0:T(8,128)S(1)}, u32[]{:S(2)}, u32[]{:S(2)}) %collective-permute-start.4) | collective-permute-done | bytes 32800 | tf_op jit(solution)/shard_map/ppermute | solution.py:244
  66.7 0.8 %broadcast_select_fusion.1 = (f32[64,128]{1,0:T(8,128)S(1)}, f32[64,128]{1,0:T(8,128)S(1)}) fusion(f32[64,128]{1,0:T(8,128)} %shard_map.50, f32[64,128]{1,0:T(8,128)S(1)} %collective-permute-done.4, pred[]{:T(512)S(6)} %eq.3), kind=kLoop, calls=%fused_computation.4 | loop fusion | flops 16384 | bytes 131073 | tf_op jit(solution)/shard_map/jit(_where)/select_n | solution.py:245
  67.4 0.7 select_bitcast_fusion
Async XLA Ops:
  0.6 16.0 %collective-permute-start.1 = (f32[128,128]{1,0:T(8,128)}, f32[128,128]{1,0:T(8,128)S(1)}, u32[]{:S(2)}, u32[]{:S(2)}) collective-permute-start(f32[128,128]{1,0:T(8,128)} %bitcast.8), channel_id=1, source_target_pairs={{8,0},{10,2},{12,4},{14,6},{0,8},{2,10},{4,12},{6,14},{9,1},{11,3}... | collective-permute-start | bytes 196616 | tf_op jit(solution)/shard_map/ppermute | solution.py:217
  3.8 12.9 %collective-permute-start.2 = (f32[35,128]{1,0:T(8,128)S(1)}, f32[35,128]{1,0:T(8,128)S(1)}, u32[]{:S(2)}, u32[]{:S(2)}) collective-permute-start(f32[35,128]{1,0:T(8,128)S(1)} %constant_dynamic-slice_fusion), channel_id=1, source_target_pairs={{10,0},{12,2},{14,4},{0,10},{2,12},{4,14},{11,1},{13,3},{15,5},{1,... | collective-permute-start | bytes 53768 | tf_op jit(solution)/shard_map/ppermute | solution.py:217
  5.1 8.2 %collective-permute-start.3 = (f32[2,128]{1,0:T(2,128)S(1)}, f32[2,128]{1,0:T(2,128)S(1)}, u32[]{:S(2)}, u32[]{:S(2)}) collective-permute-start(f32[2,128]{1,0:T(2,128)S(1)} %slice_bitcast_fusion), channel_id=1, source_target_pairs={{2,8},{4,10},{6,12},{8,14},{3,9},{5,11},{7,13},{9,15},{18,24},{20,... | collective-permute-start | bytes 3080 | tf_op jit(solution)/shard_map/ppermute | solution.py:217
  11.4 5.2 %collective-permute-start = (f32[2,128]{1,0:T(2,128)S(1)}, f32[2,128]{1,0:T(2,128)S(1)}, u32[]{:S(2)}, u32[]{:S(2)}) collective-permute-start(f32[2,128]{1,0:T(2,128)S(1)} %slice_bitcast_fusion), channel_id=1, source_target_pairs={{2,0},{4,2},{6,4},{8,6},{10,8},{12,10},{14,12},{3,1},{5,3},{7,5},{... | collective-permute-start | bytes 3080 | tf_op jit(solution)/shard_map/ppermute | solution.py:217
  13.4 3.3 %copy-start.2 = (f32[2,128]{1,0:T(2,128)}, f32[2,128]{1,0:T(2,128)S(1)}, u32[]{:S(2)}) copy-start(f32[2,128]{1,0:T(2,128)S(1)} %collective-permute-done.3.last_ref) | copy-start | bytes 3076
  16.6 0.5 copy-start.3
  16.6 0.6 copy-start.1
  16.6 0.6 copy-start
  62.9 3.7 %collective-permute-start.4 = (f32[64,128]{1,0:T(8,128)}, f32[64,128]{1,0:T(8,128)S(1)}, u32[]{:S(2)}, u32[]{:S(2)}) collective-permute-start(f32[64,128]{1,0:T(8,128)} %shard_map.50), channel_id=1, source_target_pairs={{0,1},{1,0},{2,3},{3,2},{4,5},{5,4},{6,7},{7,6},{8,9},{9,8},{10,11... | collective-permute-start | bytes 98312 | tf_op jit(solution)/shard_map/ppermute | solution.py:244

commit v2 on v1

v2 whole, which is shorter than its diff:
```python
import functools

import jax
import jax.numpy as jnp
from jax import lax
from jax.experimental import pallas as pl
from jax.experimental.pallas import tpu as pltpu
from jax.sharding import PartitionSpec as P

M = 256
LANES = 128
OFF_DEV = 128
BAND_SPAN = 4096
BAND_BASE = 65536
EPS = 1e-06

WIN = M // LANES
BEFORE = BAND_SPAN // LANES + 1
AFTER = BEFORE + WIN


def window_moments(samples, scratch):
    count = samples.shape[0]
    lane = lax.broadcasted_iota(jnp.int32, samples.shape, 1)
    slots = iter(range(scratch.shape[0]))

    def ahead(values, distance):
        slot = next(slots)
        scratch[slot, pl.ds(0, count), :] = values
        below = scratch[slot, pl.ds(1, count), :]
        if distance == LANES:
            return below
        joined = jnp.where(lane < distance, below, values)
        return pltpu.roll(joined, LANES - distance, 1)

    total = samples
    spread = None
    size = 1
    while size < M:
        later = ahead(total, size)
        gap = later - total
        step = gap * gap * (0.5 / size)
        spread = step if spread is None else spread + ahead(spread, size) + step
        total = later + total
        size *= 2
    return total * (1.0 / M), spread


STEPS = 15


def profile_kernel(
    geometry,
    starts_ref,
    own_ref,
    halo_ref,
    tail_ref,
    main_ref,
    side_ref,
    last_ref,
    out_ref,
    own_s,
    pair_s,
    shifted,
    center_s,
    factor_s,
    shift_s,
    turned_s,
    sheet_s,
    pair_z_s,
):
    devices, distance, rows, tiles, role, unroll = geometry
    bands = starts_ref.shape[0]
    position = lax.axis_index("tm")
    first_row = lax.axis_index("band") * tiles if tiles < rows else 0
    is_col = position >= distance if role is None else role
    block = rows * LANES

    own_s[pl.ds(0, rows), :] = own_ref[...]
    own_s[pl.ds(rows, WIN), :] = jnp.where(position == devices - 1, tail_ref[...], halo_ref[...])

    @pl.when(jnp.logical_not(is_col))
    def _():
        pair_s[pl.ds(0, rows), :] = main_ref[...]
        pair_s[pl.ds(rows, AFTER), :] = side_ref[...]

        @pl.when(position == devices - distance - 1)
        def _():
            pair_s[pl.ds(rows, WIN), :] = tail_ref[...]

    @pl.when(is_col)
    def _():
        pair_s[pl.ds(0, BEFORE), :] = side_ref[pl.ds(WIN, BEFORE), :]
        pair_s[pl.ds(BEFORE, rows), :] = main_ref[...]
        pair_s[pl.ds(BEFORE + rows, WIN), :] = last_ref[...]

    pair_s[pl.ds(rows + AFTER, pair_s.shape[0] - rows - AFTER), :] = jnp.zeros(
        (pair_s.shape[0] - rows - AFTER, LANES), jnp.float32
    )
    lane = lax.broadcasted_iota(jnp.int32, (1, LANES), 1)
    reach = tiles + 1 + WIN
    begins = []
    for band in range(bands):
        start = starts_ref[band]
        begin = jnp.where(is_col, BEFORE * LANES - (OFF_DEV - 1) - start, start) + first_row * LANES
        begins.append(begin)
        whole, part = begin // LANES, begin % LANES
        here = pair_s[pl.ds(whole, reach), :]
        below = pair_s[pl.ds(whole + 1, reach), :]
        shifted[band, pl.ds(0, reach), :] = pltpu.roll(jnp.where(lane < part, below, here), LANES - part, 1)
    shifted[bands, pl.ds(0, reach - 1), :] = own_s[pl.ds(first_row, reach - 1), :]
    center, spread = window_moments(shifted[...].reshape(-1, LANES), shift_s)
    center_s[...] = center.reshape(center_s.shape)
    factor_s[...] = lax.rsqrt(spread + M * EPS).reshape(factor_s.shape)

    row_id = lax.broadcasted_iota(jnp.int32, (LANES, LANES), 0)
    col_id = lax.broadcasted_iota(jnp.int32, (LANES, LANES), 1)
    ahead = col_id > row_id
    near_part = col_id >= row_id

    def turned(stream, row):
        line = jnp.broadcast_to(shifted[stream, pl.ds(row, 1), :], (LANES, LANES))
        return pltpu.roll(line, 1, 1, stride=1, stride_axis=0)

    def sheet(before, after):
        return jnp.where(ahead, after, before)

    def centered(stream, tile, low, high, scale):
        center = center_s[stream, pl.ds(tile, 1), :]
        low, high = low - center, high - center
        if scale:
            factor = factor_s[stream, pl.ds(tile, 1), :]
            low, high = low * factor, high * factor
        return jnp.concatenate([low.astype(jnp.bfloat16), high.astype(jnp.bfloat16)], axis=0)

    for stream in range(bands + 1):
        first = 1 if stream < bands else 0
        lines = [turned(stream, row) for row in range(first + 2)]
        sheets = [sheet(a, b) for a, b in zip(lines, lines[1:])]
        turned_s[stream] = lines[-1]
        sheet_s[stream] = sheets[-1]
        if stream < bands:
            pair_z_s[stream] = centered(stream, 0, sheets[0], sheets[1], True)

    low_edge = BEFORE * LANES - (position - distance) * block
    high_edge = (devices - position - distance) * block
    lo = jnp.where(is_col, low_edge, 0)
    hi = jnp.where(is_col, 1 << 30, high_edge)

    def steps(masked, group, _):
        lines = [turned_s[stream] for stream in range(bands + 1)]
        sheets = [sheet_s[stream] for stream in range(bands + 1)]
        pairs = [pair_z_s[band] for band in range(bands)]
        for inner in range(unroll):
            tile = group * unroll + inner
            following = []
            for stream in range(bands + 1):
                at = tile + 1 if stream < bands else tile
                line = turned(stream, at + 2)
                high = sheet(lines[stream], line)
                following.append(centered(stream, at, sheets[stream], high, stream < bands))
                lines[stream], sheets[stream] = line, high
            best = None
            for band in range(bands):
                both = jnp.concatenate([pairs[band], following[band]], axis=1)
                scores = lax.dot_general(
                    following[bands], both, (((0,), (0,)), ((), ())), preferred_element_type=jnp.float32
                )
                if masked:
                    index = begins[band] + tile * LANES + lax.broadcasted_iota(jnp.int32, (1, 2 * LANES), 1)
                    scores = jnp.where((index >= lo) & (index < hi), scores, -1e30)
                mixed = jnp.where(near_part, scores[:, :LANES], scores[:, LANES:])
                best = mixed if best is None else jnp.maximum(best, mixed)
                pairs[band] = following[band]
            found = jnp.max(jnp.transpose(best), axis=0, keepdims=True)
            found = found * factor_s[bands, pl.ds(tile, 1), :]
            out_ref[pl.ds(tile, 1), :] = jnp.maximum(found, -1.0)
        for stream in range(bands + 1):
            turned_s[stream] = lines[stream]
            sheet_s[stream] = sheets[stream]
        for band in range(bands):
            pair_z_s[band] = pairs[band]
        return 0

    size = unroll * LANES
    groups = tiles // unroll
    first_full, last_full = jnp.int32(0), jnp.int32(groups)
    for begin in begins:
        first_full = jnp.maximum(first_full, (lo - begin + size - 1) // size)
        last_full = jnp.minimum(last_full, (hi - begin - LANES) // size)
    first_full = jnp.clip(first_full, 0, groups)
    last_full = jnp.clip(last_full, first_full, groups)
    lax.fori_loop(0, first_full, functools.partial(steps, True), 0)
    lax.fori_loop(first_full, last_full, functools.partial(steps, False), 0)
    lax.fori_loop(last_full, groups, functools.partial(steps, True), 0)


def profile(geometry, starts, own, halo, tail, main, side, last):
    devices, distance, rows, tiles, role = geometry
    bands = starts.shape[0]
    vmem = pl.BlockSpec(memory_space=pltpu.VMEM)
    pad = -(-(tiles + 2 + WIN) // 8) * 8
    unroll = UNROLL if tiles % UNROLL == 0 else 1
    return pl.pallas_call(
        functools.partial(profile_kernel, geometry + (unroll,)),
        out_shape=jax.ShapeDtypeStruct((tiles, LANES), jnp.float32),
        in_specs=[pl.BlockSpec(memory_space=pltpu.SMEM)] + [vmem] * 6,
        out_specs=vmem,
        scratch_shapes=[
            pltpu.VMEM((rows + 8, LANES), jnp.float32),
            pltpu.VMEM((-(-(rows + AFTER + 2) // 8) * 8, LANES), jnp.float32),
            pltpu.VMEM((bands + 1, pad, LANES), jnp.float32),
            pltpu.VMEM((bands + 1, pad, LANES), jnp.float32),
            pltpu.VMEM((bands + 1, pad, LANES), jnp.float32),
            pltpu.VMEM((STEPS, (bands + 1) * pad + 8, LANES), jnp.float32),
            pltpu.VMEM((bands + 1, LANES, LANES), jnp.float32),
            pltpu.VMEM((bands + 1, LANES, LANES), jnp.float32),
            pltpu.VMEM((bands, M, LANES), jnp.bfloat16),
        ],
    )(starts, own, halo, tail, main, side, last)


def body(split, series, tail, band_starts):
    block_len = series.shape[0]
    rows = block_len // LANES
    devices = lax.axis_size("tm")
    distance = BAND_BASE // block_len
    cores = lax.axis_size("band") if split else 1
    tiles = rows // cores
    position = lax.axis_index("tm")
    own = series.reshape(rows, LANES)
    tail = tail.reshape(WIN, LANES)
    head = own[:WIN]

    def move(value, steps):
        route = [(d - s, d) for d, s in steps if 0 <= d - s < devices]
        return lax.ppermute(value, "tm", route)

    everyone = range(devices)
    halo = move(head, [(d, -1) for d in everyone])
    row_side = [d for d in everyone if d < devices - distance]
    col_side = [d for d in everyone if d >= distance]
    last = move(head, [(d, distance - 1) for d in col_side])
    if devices <= 2 * distance:
        main = move(own, [(d, -distance) for d in row_side] + [(d, distance) for d in col_side])
        begin = jnp.where(position >= distance, 0, rows - AFTER)
        piece = lax.dynamic_slice_in_dim(own, begin, AFTER)
        side = move(piece, [(d, -distance - 1) for d in row_side] + [(d, distance + 1) for d in col_side])
        found = [profile((devices, distance, rows, tiles, None), band_starts, own, halo, tail, main, side, last)]
    else:
        main = move(own, [(d, -distance) for d in row_side])
        side = move(own[:AFTER], [(d, -distance - 1) for d in row_side])
        found = [profile((devices, distance, rows, tiles, False), band_starts, own, halo, tail, main, side, last)]
        main = move(own, [(d, distance) for d in col_side])
        side = move(own[rows - AFTER :], [(d, distance + 1) for d in col_side])
        found.append(
            profile((devices, distance, rows, tiles, True), band_starts, own, halo, tail, main, side, last)
        )
    if cores > 1:
        ring = [(i, (i + 1) % cores) for i in range(cores)]
        first = lax.axis_index("band") == 0
        whole = []
        for part in found:
            other = lax.ppermute(part, "band", ring)
            whole.append(jnp.concatenate([jnp.where(first, part, other), jnp.where(first, other, part)]))
        found = whole
    is_row, is_col = position < devices - distance, position >= distance
    row_best = jnp.where(is_row, found[0], -1.0)
    col_best = jnp.where(is_col, found[-1], -1.0)
    return row_best.reshape(-1), col_best.reshape(-1)


SPLIT = True
UNROLL = 4


def solution(mesh):
    placed = (P(("groups", "tm")), P("groups"), P("groups"))
    split = SPLIT and mesh.shape["band"] == 2
    return jax.shard_map(
        functools.partial(body, split),
        mesh=mesh,
        in_specs=placed,
        out_specs=(P(("groups", "tm")), P(("groups", "tm"))),
        check_vma=False,
    )
```

time: 68.5 us -> 36.8 us (0.54)
  Pallas kernels: 45.7 us -> 13.9 us
    pallas_call x1, Pallas kernels: 45.7 us -> 13.9 us  [profile(): pl.pallas_call(functools.partial(profile_kernel, geometry + (unroll,)), o...]
  transfers between devices with their start and end apart: 5 -> 5, of which waited for: 2 -> 2; matrix products, arithmetic and copies ran while one was open for 2% -> 4% of each run, Pallas kernels for 0% -> 0%
where the time goes in v2:
time: 36.8 us; the launch traced here: 36.4 us
  starting transfers between devices  13.9 us (38%)
  Pallas kernels  13.9 us (38%)
  waiting for transfers between devices  4.35 us (12%)
  local copies, waits for them, and re-layouts  2.08 us (6%)
  other arithmetic  1.43 us (4%)
  between operations  0.7 us (2%)
    pallas_call x1, Pallas kernels, profile(): pl.pallas_call(functools.partial(profile_kernel, geometry + (unroll,)), o...  13.9 us
    ppermute x4, starting transfers between devices, move(): return lax.ppermute(value, 'tm', route)  11.2 us
    ppermute x4, waiting for transfers between devices, move(): return lax.ppermute(value, 'tm', route)  3.28 us
    ppermute x1, starting transfers between devices, body(): other = lax.ppermute(part, 'band', ring)  2.67 us
    ppermute x1, waiting for transfers between devices, body(): other = lax.ppermute(part, 'band', ring)  1.07 us
    dynamic_slice x1, local copies, waits for them, and re-layouts, body(): piece = lax.dynamic_slice_in_dim(own, begin, AFTER)  0.77 us
    select_n x1, other arithmetic, body(): jnp.where(first, part, other)  0.76 us
  transfers between devices with their start and end apart: 5, of which 2 were waited for; matrix products, arithmetic and copies ran while one was open for 4% of the time, Pallas kernels for 0%

profile of v2, /device:TPU:13, one launch (start us, length us, event | category | flops | bytes accessed | tf_op | source)
XLA Modules:
  0.0 36.4 jit_solution(8639369837194456851)
XLA Ops:
  0.6 2.4 %collective-permute-start.1 = (f32[128,128]{1,0:T(8,128)}, f32[128,128]{1,0:T(8,128)S(1)}, u32[]{:S(2)}, u32[]{:S(2)}) collective-permute-start(f32[128,128]{1,0:T(8,128)} %bitcast.8), channel_id=1, source_target_pairs={{8,0},{10,2},{12,4},{14,6},{0,8},{2,10},{4,12},{6,14},{9,1},{11,3}... | collective-permute-start | bytes 196616 | tf_op jit(solution)/shard_map/ppermute | solution.py:237
  3.0 0.8 %constant_dynamic-slice_fusion = f32[35,128]{1,0:T(8,128)S(1)} fusion(f32[128,128]{1,0:T(8,128)} %bitcast.9, s32[]{:T(128)S(6)} %select_n.41), kind=kLoop, calls=%fused_computation.6 | loop fusion | bytes 35844 | tf_op jit(solution)/shard_map/dynamic_slice | solution.py:247
  3.8 0.7 %collective-permute-start.2 = (f32[35,128]{1,0:T(8,128)S(1)}, f32[35,128]{1,0:T(8,128)S(1)}, u32[]{:S(2)}, u32[]{:S(2)}) collective-permute-start(f32[35,128]{1,0:T(8,128)S(1)} %constant_dynamic-slice_fusion), channel_id=1, source_target_pairs={{10,0},{12,2},{14,4},{0,10},{2,12},{4,14},{11,1},{13,3},{15,5},{1,... | collective-permute-start | bytes 53768 | tf_op jit(solution)/shard_map/ppermute | solution.py:237
  4.4 0.7 %slice_bitcast_fusion = f32[2,128]{1,0:T(2,128)S(1)} fusion(f32[16384]{0:T(1024)} %param.3), kind=kLoop, calls=%fused_computation.5 | loop fusion | bytes 2048 | tf_op jit(solution)/shard_map/slice | solution.py:233
  5.1 6.3 %collective-permute-start.3 = (f32[2,128]{1,0:T(2,128)S(1)}, f32[2,128]{1,0:T(2,128)S(1)}, u32[]{:S(2)}, u32[]{:S(2)}) collective-permute-start(f32[2,128]{1,0:T(2,128)S(1)} %slice_bitcast_fusion), channel_id=1, source_target_pairs={{2,8},{4,10},{6,12},{8,14},{3,9},{5,11},{7,13},{9,15},{18,24},{20,... | collective-permute-start | bytes 3080 | tf_op jit(solution)/shard_map/ppermute | solution.py:237
  11.4 1.9 %collective-permute-start = (f32[2,128]{1,0:T(2,128)S(1)}, f32[2,128]{1,0:T(2,128)S(1)}, u32[]{:S(2)}, u32[]{:S(2)}) collective-permute-start(f32[2,128]{1,0:T(2,128)S(1)} %slice_bitcast_fusion), channel_id=1, source_target_pairs={{2,0},{4,2},{6,4},{8,6},{10,8},{12,10},{14,12},{3,1},{5,3},{7,5},{... | collective-permute-start | bytes 3080 | tf_op jit(solution)/shard_map/ppermute | solution.py:237
  13.3 0.0 collective-permute-done.3.last_ref
  13.4 0.0 copy-start.2
  13.4 3.3 %collective-permute-done.halo_ref = f32[2,128]{1,0:T(2,128)S(1)} collective-permute-done((f32[2,128]{1,0:T(2,128)S(1)}, f32[2,128]{1,0:T(2,128)S(1)}, u32[]{:S(2)}, u32[]{:S(2)}) %collective-permute-start) | collective-permute-done | bytes 1056 | tf_op jit(solution)/shard_map/ppermute | solution.py:237
  16.6 0.0 copy-start.3
  16.6 0.0 collective-permute-done.2.side_ref
  16.6 0.0 copy-start.1
  16.6 0.0 collective-permute-done.1.main_ref
  16.6 0.0 copy-start
  16.7 0.0 copy-done.2
  16.7 0.5 %copy-done.3 = f32[2,128]{1,0:T(2,128)} copy-done((f32[2,128]{1,0:T(2,128)}, f32[2,128]{1,0:T(2,128)S(1)}, u32[]{:S(2)}) %copy-start.3) | copy-done | bytes 1048
  17.2 0.1 copy-done.1
  17.2 0.0 copy-done
  17.3 13.9 %shard_map.50 = f32[64,128]{1,0:T(8,128)} custom-call(s32[2]{0:T(128)} %starts_ref.1, f32[128,128]{1,0:T(8,128)} %bitcast.10, f32[2,128]{1,0:T(2,128)} %copy-done.3, f32[2,128]{1,0:T(2,128)} %bitcast.11, f32[128,128]{1,0:T(8,128)} %copy-done, f32[35,128]{1,0:T(8,128)} %copy-done.1, f32[2,128]{1,0:T(2,128)} %copy-done.2), custom_call_target="tpu_custom_call" | custom-call | tf_op jit(solution)/shard_map/pallas_call | solution.py:204
  31.2 2.7 %collective-permute-start.4 = (f32[64,128]{1,0:T(8,128)}, f32[64,128]{1,0:T(8,128)S(1)}, u32[]{:S(2)}, u32[]{:S(2)}) collective-permute-start(f32[64,128]{1,0:T(8,128)} %shard_map.50), channel_id=1, source_target_pairs={{0,1},{1,0},{2,3},{3,2},{4,5},{5,4},{6,7},{7,6},{8,9},{9,8},{10,11... | collective-permute-start | bytes 98312 | tf_op jit(solution)/shard_map/ppermute | solution.py:264
  33.9 1.1 %collective-permute-done.4 = f32[64,128]{1,0:T(8,128)S(1)} collective-permute-done((f32[64,128]{1,0:T(8,128)}, f32[64,128]{1,0:T(8,128)S(1)}, u32[]{:S(2)}, u32[]{:S(2)}) %collective-permute-start.4) | collective-permute-done | bytes 32800 | tf_op jit(solution)/shard_map/ppermute | solution.py:264
  35.0 0.8 %broadcast_select_fusion.1 = (f32[64,128]{1,0:T(8,128)S(1)}, f32[64,128]{1,0:T(8,128)S(1)}) fusion(f32[64,128]{1,0:T(8,128)} %shard_map.50, f32[64,128]{1,0:T(8,128)S(1)} %collective-permute-done.4, pred[]{:T(512)S(6)} %eq.3), kind=kLoop, calls=%fused_computation.4 | loop fusion | flops 16384 | bytes 131073 | tf_op jit(solution)/shard_map/jit(_where)/select_n | solution.py:265
  35.7 0.7 %select_bitcast_fusion = (f32[16384]{0:T(1024)}, f32[16384]{0:T(1024)}) fusion(f32[64,128]{1,0:T(8,128)S(1)} %get-tuple-element.5, f32[64,128]{1,0:T(8,128)S(1)} %get-tuple-element.4, pred[]{:T(512)S(6)} %ge.4, pred[]{:T(512)S(6)} %lt.4), kind=kLoop, calls=%fused_computation.1 | loop fusion | flops 49152 | bytes 196610 | tf_op jit(solution)/shard_map/jit(_where)/select_n | solution.py:269
Async XLA Ops:
  0.6 16.0 %collective-permute-start.1 = (f32[128,128]{1,0:T(8,128)}, f32[128,128]{1,0:T(8,128)S(1)}, u32[]{:S(2)}, u32[]{:S(2)}) collective-permute-start(f32[128,128]{1,0:T(8,128)} %bitcast.8), channel_id=1, source_target_pairs={{8,0},{10,2},{12,4},{14,6},{0,8},{2,10},{4,12},{6,14},{9,1},{11,3}... | collective-permute-start | bytes 196616 | tf_op jit(solution)/shard_map/ppermute | solution.py:237
  3.8 12.9 %collective-permute-start.2 = (f32[35,128]{1,0:T(8,128)S(1)}, f32[35,128]{1,0:T(8,128)S(1)}, u32[]{:S(2)}, u32[]{:S(2)}) collective-permute-start(f32[35,128]{1,0:T(8,128)S(1)} %constant_dynamic-slice_fusion), channel_id=1, source_target_pairs={{10,0},{12,2},{14,4},{0,10},{2,12},{4,14},{11,1},{13,3},{15,5},{1,... | collective-permute-start | bytes 53768 | tf_op jit(solution)/shard_map/ppermute | solution.py:237
  5.1 8.2 %collective-permute-start.3 = (f32[2,128]{1,0:T(2,128)S(1)}, f32[2,128]{1,0:T(2,128)S(1)}, u32[]{:S(2)}, u32[]{:S(2)}) collective-permute-start(f32[2,128]{1,0:T(2,128)S(1)} %slice_bitcast_fusion), channel_id=1, source_target_pairs={{2,8},{4,10},{6,12},{8,14},{3,9},{5,11},{7,13},{9,15},{18,24},{20,... | collective-permute-start | bytes 3080 | tf_op jit(solution)/shard_map/ppermute | solution.py:237
  11.4 5.2 %collective-permute-start = (f32[2,128]{1,0:T(2,128)S(1)}, f32[2,128]{1,0:T(2,128)S(1)}, u32[]{:S(2)}, u32[]{:S(2)}) collective-permute-start(f32[2,128]{1,0:T(2,128)S(1)} %slice_bitcast_fusion), channel_id=1, source_target_pairs={{2,0},{4,2},{6,4},{8,6},{10,8},{12,10},{14,12},{3,1},{5,3},{7,5},{... | collective-permute-start | bytes 3080 | tf_op jit(solution)/shard_map/ppermute | solution.py:237
  13.4 3.3 %copy-start.2 = (f32[2,128]{1,0:T(2,128)}, f32[2,128]{1,0:T(2,128)S(1)}, u32[]{:S(2)}) copy-start(f32[2,128]{1,0:T(2,128)S(1)} %collective-permute-done.3.last_ref) | copy-start | bytes 3076
  16.6 0.5 %copy-start.3 = (f32[2,128]{1,0:T(2,128)}, f32[2,128]{1,0:T(2,128)S(1)}, u32[]{:S(2)}) copy-start(f32[2,128]{1,0:T(2,128)S(1)} %collective-permute-done.halo_ref) | copy-start | bytes 3076
  16.6 0.6 %copy-start.1 = (f32[35,128]{1,0:T(8,128)}, f32[35,128]{1,0:T(8,128)S(1)}, u32[]{:S(2)}) copy-start(f32[35,128]{1,0:T(8,128)S(1)} %collective-permute-done.2.side_ref) | copy-start | bytes 53764
  16.6 0.6 %copy-start = (f32[128,128]{1,0:T(8,128)}, f32[128,128]{1,0:T(8,128)S(1)}, u32[]{:S(2)}) copy-start(f32[128,128]{1,0:T(8,128)S(1)} %collective-permute-done.1.main_ref) | copy-start | bytes 196612
  31.2 3.7 %collective-permute-start.4 = (f32[64,128]{1,0:T(8,128)}, f32[64,128]{1,0:T(8,128)S(1)}, u32[]{:S(2)}, u32[]{:S(2)}) collective-permute-start(f32[64,128]{1,0:T(8,128)} %shard_map.50), channel_id=1, source_target_pairs={{0,1},{1,0},{2,3},{3,2},{4,5},{5,4},{6,7},{7,6},{8,9},{9,8},{10,11... | collective-permute-start | bytes 98312 | tf_op jit(solution)/shard_map/ppermute | solution.py:264

commit v3 on v2

v3 whole, which is shorter than its diff:
```python
import functools

import jax
import jax.numpy as jnp
from jax import lax
from jax.experimental import pallas as pl
from jax.experimental.pallas import tpu as pltpu
from jax.sharding import PartitionSpec as P

M = 256
LANES = 128
OFF_DEV = 128
BAND_SPAN = 4096
BAND_BASE = 65536
EPS = 1e-06

WIN = M // LANES
BEFORE = BAND_SPAN // LANES + 1
AFTER = BEFORE + WIN


def window_moments(samples, scratch):
    count = samples.shape[0]
    lane = lax.broadcasted_iota(jnp.int32, samples.shape, 1)
    slots = iter(range(scratch.shape[0]))

    def ahead(values, distance):
        slot = next(slots)
        scratch[slot, pl.ds(0, count), :] = values
        below = scratch[slot, pl.ds(1, count), :]
        if distance == LANES:
            return below
        joined = jnp.where(lane < distance, below, values)
        return pltpu.roll(joined, LANES - distance, 1)

    total = samples
    spread = None
    size = 1
    while size < M:
        later = ahead(total, size)
        gap = later - total
        step = gap * gap * (0.5 / size)
        spread = step if spread is None else spread + ahead(spread, size) + step
        total = later + total
        size *= 2
    return total * (1.0 / M), spread


STEPS = 15


def tile_masks():
    row_id = lax.broadcasted_iota(jnp.int32, (LANES, LANES), 0)
    col_id = lax.broadcasted_iota(jnp.int32, (LANES, LANES), 1)
    return col_id > row_id, col_id >= row_id


def turned(line):
    return pltpu.roll(jnp.broadcast_to(line, (LANES, LANES)), 1, 1, stride=1, stride_axis=0)


def sheet(before, after, ahead):
    return jnp.where(ahead, after, before)


def centered(low, high, center, factor=None):
    low, high = low - center, high - center
    if factor is not None:
        low, high = low * factor, high * factor
    return jnp.concatenate([low.astype(jnp.bfloat16), high.astype(jnp.bfloat16)], axis=0)


def own_kernel(tiles, unroll, own_ref, z_ref, factor_ref, rows_s, center_s, shift_s, turned_s, sheet_s):
    first_row = lax.axis_index("band") * tiles
    count = rows_s.shape[0]
    rows_s[pl.ds(tiles, count - tiles), :] = jnp.zeros((count - tiles, LANES), jnp.float32)
    rows_s[pl.ds(0, tiles), :] = own_ref[pl.ds(first_row, tiles), :]

    @pl.when(first_row == 0)
    def _():
        rows_s[pl.ds(tiles, WIN), :] = own_ref[pl.ds(tiles, WIN), :]

    center, spread = window_moments(rows_s[...], shift_s)
    center_s[...] = center
    factor_ref[...] = lax.rsqrt(spread + M * EPS)[:tiles]
    ahead, _ = tile_masks()
    first, second = (turned(rows_s[pl.ds(row, 1), :]) for row in range(2))
    turned_s[...] = second
    sheet_s[...] = sheet(first, second, ahead)

    def group(index, _):
        line, low = turned_s[...], sheet_s[...]
        for inner in range(unroll):
            tile = index * unroll + inner
            after = turned(rows_s[pl.ds(tile + 2, 1), :])
            high = sheet(line, after, ahead)
            z_ref[tile] = jnp.transpose(centered(low, high, center_s[pl.ds(tile, 1), :]))
            line, low = after, high
        turned_s[...] = line
        sheet_s[...] = low
        return 0

    lax.fori_loop(0, tiles // unroll, group, 0)


def own_side(tiles, own):
    vmem = pl.BlockSpec(memory_space=pltpu.VMEM)
    count = -(-(tiles + WIN) // 8) * 8
    return pl.pallas_call(
        functools.partial(own_kernel, tiles, UNROLL),
        out_shape=(
            jax.ShapeDtypeStruct((tiles, LANES, M), jnp.bfloat16),
            jax.ShapeDtypeStruct((tiles, LANES), jnp.float32),
        ),
        in_specs=[vmem],
        out_specs=(vmem, vmem),
        scratch_shapes=[
            pltpu.VMEM((count, LANES), jnp.float32),
            pltpu.VMEM((count, LANES), jnp.float32),
            pltpu.VMEM((STEPS, count + 8, LANES), jnp.float32),
            pltpu.VMEM((LANES, LANES), jnp.float32),
            pltpu.VMEM((LANES, LANES), jnp.float32),
        ],
        compiler_params=pltpu.CompilerParams(vmem_limit_bytes=VMEM_LIMIT),
        cost_estimate=pl.CostEstimate(flops=20 * tiles * LANES * M, transcendentals=0, bytes_accessed=2 * tiles * LANES * M),
    )(own)


def profile_kernel(
    geometry,
    starts_ref,
    own_ref,
    halo_ref,
    tail_ref,
    main_ref,
    side_ref,
    factor_ref,
    z_ref,
    out_ref,
    late_z_s,
    late_s,
    pair_s,
    shifted,
    center_s,
    factor_s,
    shift_s,
    turned_s,
    sheet_s,
    pair_z_s,
    best_s,
):
    devices, distance, rows, tiles, role, unroll = geometry
    bands = starts_ref.shape[0]
    position = lax.axis_index("tm")
    core = lax.axis_index("band")
    is_col = position >= distance if role is None else jnp.bool_(role)
    block = rows * LANES
    groups = tiles // unroll
    early = tiles - WIN

    pair_s[pl.ds(tiles + AFTER, pair_s.shape[0] - tiles - AFTER), :] = jnp.zeros(
        (pair_s.shape[0] - tiles - AFTER, LANES), jnp.float32
    )

    @pl.when(jnp.logical_not(is_col) & (core == 0))
    def _():
        pair_s[pl.ds(0, tiles + AFTER), :] = main_ref[pl.ds(0, tiles + AFTER), :]

    @pl.when(jnp.logical_not(is_col) & (core != 0))
    def _():
        pair_s[pl.ds(0, tiles), :] = main_ref[pl.ds(rows - tiles, tiles), :]
        pair_s[pl.ds(tiles, AFTER), :] = side_ref[...]

        @pl.when(position == devices - distance - 1)
        def _():
            pair_s[pl.ds(tiles, WIN), :] = tail_ref[...]

    @pl.when(is_col & (core == 0))
    def _():
        pair_s[pl.ds(0, BEFORE), :] = side_ref[pl.ds(WIN, BEFORE), :]
        pair_s[pl.ds(BEFORE, tiles + WIN), :] = main_ref[pl.ds(0, tiles + WIN), :]

    @pl.when(is_col & (core != 0))
    def _():
        pair_s[pl.ds(0, tiles + BEFORE), :] = main_ref[pl.ds(rows - tiles - BEFORE, tiles + BEFORE), :]
        pair_s[pl.ds(tiles + BEFORE, WIN), :] = side_ref[pl.ds(0, WIN), :]

    @pl.when(core == 0)
    def _():
        late_s[pl.ds(0, 2 * WIN), :] = own_ref[pl.ds(early, 2 * WIN), :]

    @pl.when(core != 0)
    def _():
        late_s[pl.ds(0, WIN), :] = own_ref[pl.ds(rows - WIN, WIN), :]
        late_s[pl.ds(WIN, WIN), :] = jnp.where(position == devices - 1, tail_ref[...], halo_ref[pl.ds(0, WIN), :])

    lane = lax.broadcasted_iota(jnp.int32, (1, LANES), 1)
    reach = tiles + 1 + WIN
    begins = []
    for band in range(bands):
        start = starts_ref[band]
        begin = jnp.where(is_col, BEFORE * LANES - (OFF_DEV - 1) - start, start)
        begins.append(begin)
        whole, part = begin // LANES, begin % LANES
        here = pair_s[pl.ds(whole, reach), :]
        below = pair_s[pl.ds(whole + 1, reach), :]
        shifted[band, pl.ds(0, reach), :] = pltpu.roll(jnp.where(lane < part, below, here), LANES - part, 1)
    center, spread = window_moments(shifted[...].reshape(-1, LANES), shift_s)
    center_s[...] = center.reshape(center_s.shape)
    factor_s[...] = lax.rsqrt(spread + M * EPS).reshape(factor_s.shape)
    late_center, late_spread = window_moments(late_s[...], shift_s)
    late_factor = lax.rsqrt(late_spread + M * EPS)

    ahead, near_part = tile_masks()

    for band in range(bands):
        lines = [turned(shifted[band, pl.ds(row, 1), :]) for row in range(WIN + 1)]
        sheets = [sheet(a, b, ahead) for a, b in zip(lines, lines[1:])]
        turned_s[band] = lines[-1]
        sheet_s[band] = sheets[-1]
        pair_z_s[band] = centered(*sheets, center_s[band, pl.ds(0, 1), :], factor_s[band, pl.ds(0, 1), :])

    shift = core * tiles * LANES
    low_edge = BEFORE * LANES - (position - distance) * block - shift
    high_edge = (devices - position - distance) * block - shift
    lo = jnp.where(is_col, low_edge, 0)
    hi = jnp.where(is_col, 1 << 30, high_edge)

    lines = [turned(late_s[pl.ds(row, 1), :]) for row in range(2 * WIN)]
    sheets = [sheet(a, b, ahead) for a, b in zip(lines, lines[1:])]
    for tile in range(WIN):
        late_z_s[tile] = jnp.transpose(centered(sheets[tile], sheets[tile + 1], late_center[tile : tile + 1]))

    def steps(masked, group, _):
        lines = [turned_s[band] for band in range(bands)]
        sheets = [sheet_s[band] for band in range(bands)]
        pairs = [pair_z_s[band] for band in range(bands)]
        for inner in range(unroll):
            tile = group * unroll + inner
            own = z_ref[tile]
            if inner >= unroll - WIN:
                own = jnp.where(group == groups - 1, late_z_s[inner + WIN - unroll], own)
            best = None
            for band in range(bands):
                at = tile + 1
                line = turned(shifted[band, pl.ds(at + WIN, 1), :])
                high = sheet(lines[band], line, ahead)
                following = centered(
                    sheets[band], high, center_s[band, pl.ds(at, 1), :], factor_s[band, pl.ds(at, 1), :]
                )
                lines[band], sheets[band] = line, high
                both = jnp.concatenate([pairs[band], following], axis=1)
                pairs[band] = following
                scores = jnp.dot(own, both, preferred_element_type=jnp.float32)
                if masked:
                    index = begins[band] + tile * LANES + lax.broadcasted_iota(jnp.int32, (1, 2 * LANES), 1)
                    scores = jnp.where((index >= lo) & (index < hi), scores, -1e30)
                mixed = jnp.where(near_part, scores[:, :LANES], scores[:, LANES:])
                best = mixed if best is None else jnp.maximum(best, mixed)
            found = jnp.max(best, axis=1, keepdims=True)
            best_s[...] = jnp.where(lane == tile, found, best_s[...])
        for band in range(bands):
            turned_s[band] = lines[band]
            sheet_s[band] = sheets[band]
            pair_z_s[band] = pairs[band]
        return 0

    size = unroll * LANES
    first_full, last_full = jnp.int32(0), jnp.int32(groups)
    for begin in begins:
        first_full = jnp.maximum(first_full, (lo - begin + size - 1) // size)
        last_full = jnp.minimum(last_full, (hi - begin - LANES) // size)
    first_full = jnp.clip(first_full, 0, groups)
    last_full = jnp.clip(last_full, first_full, groups)
    lax.fori_loop(0, first_full, functools.partial(steps, True), 0)
    lax.fori_loop(first_full, last_full, functools.partial(steps, False), 0)
    lax.fori_loop(last_full, groups, functools.partial(steps, True), 0)
    found = jnp.transpose(best_s[...])[:tiles]
    out_ref[...] = jnp.maximum(found * factor_ref[...], -1.0)
    late = jnp.maximum(found[early:] * late_factor[:WIN], -1.0)
    out_ref[pl.ds(early, WIN), :] = late


def profile(geometry, starts, own, halo, tail, main, side, factor, z):
    devices, distance, rows, tiles, role = geometry
    bands = starts.shape[0]
    vmem = pl.BlockSpec(memory_space=pltpu.VMEM)
    pad = -(-(tiles + 2 + WIN) // 8) * 8
    return pl.pallas_call(
        functools.partial(profile_kernel, geometry + (UNROLL,)),
        out_shape=jax.ShapeDtypeStruct((tiles, LANES), jnp.float32),
        in_specs=[pl.BlockSpec(memory_space=pltpu.SMEM)] + [vmem] * 7,
        out_specs=vmem,
        scratch_shapes=[
            pltpu.VMEM((WIN, LANES, M), jnp.bfloat16),
            pltpu.VMEM((8, LANES), jnp.float32),
            pltpu.VMEM((-(-(tiles + AFTER + 8) // 8) * 8, LANES), jnp.float32),
            pltpu.VMEM((bands, pad, LANES), jnp.float32),
            pltpu.VMEM((bands, pad, LANES), jnp.float32),
            pltpu.VMEM((bands, pad, LANES), jnp.float32),
            pltpu.VMEM((STEPS, bands * pad + 8, LANES), jnp.float32),
            pltpu.VMEM((bands, LANES, LANES), jnp.float32),
            pltpu.VMEM((bands, LANES, LANES), jnp.float32),
            pltpu.VMEM((bands, M, LANES), jnp.bfloat16),
            pltpu.VMEM((LANES, LANES), jnp.float32),
        ],
        compiler_params=pltpu.CompilerParams(vmem_limit_bytes=VMEM_LIMIT),
    )(starts, own, halo, tail, main, side, factor, z)


def body(series, tail, band_starts):
    block_len = series.shape[0]
    rows = block_len // LANES
    devices, cores = lax.axis_size("tm"), lax.axis_size("band")
    distance = BAND_BASE // block_len
    tiles = rows // cores
    position, core = lax.axis_index("tm"), lax.axis_index("band")
    own = series.reshape(rows, LANES)
    tail = tail.reshape(WIN, LANES)

    def move(value, steps):
        route = [
            ((d + s) * cores + c, d * cores + c) for d, c, s in steps if 0 <= d + s < devices
        ]
        return lax.ppermute(value, ("tm", "band"), route)

    row_side = range(devices - distance)
    col_side = range(distance, devices)
    main_row = [(d, c, distance) for d in row_side for c in range(cores)]
    main_col = [(d, c, -distance) for d in col_side for c in range(cores)]
    side_row = [(d, 1, distance + 1) for d in row_side]
    side_col = [(d, 0, -distance - 1) for d in col_side] + [(d, 1, 1 - distance) for d in col_side]
    merged = devices <= 2 * distance
    roles = [(None, main_row + main_col, side_row + side_col)] if merged else [
        (False, main_row, side_row),
        (True, main_col, side_col),
    ]
    mains = [move(own, pairs) for _, pairs, _ in roles]
    edge = lax.dynamic_slice_in_dim(own, jnp.where(core == 0, rows - AFTER, 0), AFTER)
    sides = [move(edge, pairs) for _, _, pairs in roles]
    halo = move(edge, [(d, 1, 1) for d in range(devices)])
    z, factor = own_side(tiles, own)
    found = []
    for (role, _, _), main, side in zip(roles, mains, sides):
        part = profile((devices, distance, rows, tiles, role), band_starts, own, halo, tail, main, side, factor, z)
        other = lax.ppermute(part, "band", [(0, 1), (1, 0)])
        mine = jnp.arange(cores)[:, None, None] == core
        found.append(jnp.where(mine, part[None], other[None]).reshape(-1))
    row_best = jnp.where(position < devices - distance, found[0], -1.0)
    col_best = jnp.where(position >= distance, found[-1], -1.0)
    return row_best, col_best


UNROLL = 8
VMEM_LIMIT = 24 << 20


def solution(mesh):
    placed = (P(("groups", "tm")), P("groups"), P("groups"))
    return jax.shard_map(
        body,
        mesh=mesh,
        in_specs=placed,
        out_specs=(P(("groups", "tm")), P(("groups", "tm"))),
        check_vma=False,
    )
```

time: 36.8 us -> 29.5 us (0.80)
  the two profiles are of different devices: /device:TPU:13 before, /device:TPU:5 now
where the time goes in v3:
time: 29.5 us; the launch traced here: 29.2 us
  Pallas kernels  14 us (47%)
  starting transfers between devices  9.63 us (33%)
  local copies, waits for them, and re-layouts  2.94 us (10%)
  waiting for transfers between devices  1.18 us (4%)
  other arithmetic  0.74 us (3%)
  between operations  0.73 us (2%)
    ppermute x3, starting transfers between devices, move(): return lax.ppermute(value, ('tm', 'band'), route)  9.56 us
    pallas_call x1, Pallas kernels, profile(): pl.pallas_call(functools.partial(profile_kernel, geometry + (UNROLL,)), o...  8.39 us
    pallas_call x1, Pallas kernels, own_side(): pl.pallas_call(functools.partial(own_kernel, tiles, UNROLL), out_shape=(j...  5.6 us
    unnamed x6, local copies, waits for them, and re-layouts  2.16 us
    ppermute x1, waiting for transfers between devices, body(): other = lax.ppermute(part, 'band', [(0, 1), (1, 0)])  1.17 us
    dynamic_slice x1, local copies, waits for them, and re-layouts, body(): lax.dynamic_slice_in_dim(own, jnp.where(core == 0, rows - AFTER, 0), AFTER)  0.78 us
    select_n x1, other arithmetic, body(): col_best = jnp.where(position >= distance, found[-1], -1.0)  0.73 us
  transfers between devices with their start and end apart: 4, of which 1 were waited for; matrix products, arithmetic and copies ran while one was open for 3% of the time, Pallas kernels for 19%

profile of v3, /device:TPU:5, one launch (start us, length us, event | category | flops | bytes accessed | tf_op | source)
XLA Modules:
  0.0 29.2 jit_solution(17945760684849534693)
XLA Ops:
  0.6 2.4 %collective-permute-start.1 = (f32[128,128]{1,0:T(8,128)}, f32[128,128]{1,0:T(8,128)S(1)}, u32[]{:S(2)}, u32[]{:S(2)}) collective-permute-start(f32[128,128]{1,0:T(8,128)} %bitcast.4), channel_id=1, source_target_pairs={{8,0},{9,1},{10,2},{11,3},{12,4},{13,5},{14,6},{15,7},{0,8},{1,9},... | collective-permute-start | bytes 196616 | tf_op jit(solution)/shard_map/ppermute | solution.py:325
  3.0 0.8 %constant_dynamic-slice_fusion = f32[35,128]{1,0:T(8,128)S(1)} fusion(f32[128,128]{1,0:T(8,128)} %bitcast.5, s32[]{:T(128)S(6)} %select_n.32), kind=kLoop, calls=%fused_computation.3 | loop fusion | bytes 35844 | tf_op jit(solution)/shard_map/dynamic_slice | solution.py:339
  3.8 2.1 %collective-permute-start = (f32[35,128]{1,0:T(8,128)S(1)}, f32[35,128]{1,0:T(8,128)S(1)}, u32[]{:S(2)}, u32[]{:S(2)}) collective-permute-start(f32[35,128]{1,0:T(8,128)S(1)} %constant_dynamic-slice_fusion), channel_id=1, source_target_pairs={{3,1},{5,3},{7,5},{9,7},{11,9},{13,11},{15,13},{19,17},{21,19},{23... | collective-permute-start | bytes 53768 | tf_op jit(solution)/shard_map/ppermute | solution.py:325
  5.9 5.1 %collective-permute-start.2 = (f32[35,128]{1,0:T(8,128)S(1)}, f32[35,128]{1,0:T(8,128)S(1)}, u32[]{:S(2)}, u32[]{:S(2)}) collective-permute-start(f32[35,128]{1,0:T(8,128)S(1)} %constant_dynamic-slice_fusion), channel_id=1, source_target_pairs={{11,1},{13,3},{15,5},{0,10},{2,12},{4,14},{3,9},{5,11},{7,13},{9,1... | collective-permute-start | bytes 53768 | tf_op jit(solution)/shard_map/ppermute | solution.py:325
  11.0 0.0 copy-start
  11.0 0.8 %copy-done = f32[16384]{0:T(1024)S(1)} copy-done((f32[16384]{0:T(1024)S(1)}, f32[16384]{0:T(1024)}, u32[]{:S(2)}) %copy-start) | copy-done | bytes 65560
  11.8 5.6 %shard_map.50 = (bf16[64,128,256]{2,1,0:T(8,128)(2,1)S(1)}, f32[64,128]{1,0:T(8,128)S(1)}) custom-call(f32[128,128]{1,0:T(8,128)S(1)} %bitcast.6), custom_call_target="tpu_custom_call" | custom-call | flops 41943040 | bytes 4194304 | tf_op jit(solution)/shard_map/pallas_call | solution.py:109
  17.4 0.0 collective-permute-done.halo_ref
  17.4 0.0 collective-permute-done.2.side_ref
  17.5 0.0 collective-permute-done.1.main_ref
  17.5 0.0 copy-start.1
  17.5 0.7 %copy-done.1 = f32[256]{0:T(256)S(1)} copy-done((f32[256]{0:T(256)S(1)}, f32[256]{0:T(256)}, u32[]{:S(2)}) %copy-start.1) | copy-done | bytes 1048
  18.1 0.0 copy-start.2
  18.1 0.7 %copy-done.2 = s32[2]{0:T(128)S(1)} copy-done((s32[2]{0:T(128)S(1)}, s32[2]{0:T(128)}, u32[]{:S(2)}) %copy-start.2) | copy-done | bytes 32
  18.8 8.4 %shard_map.51 = f32[64,128]{1,0:T(8,128)S(1)} custom-call(s32[2]{0:T(128)S(1)} %copy-done.2, f32[128,128]{1,0:T(8,128)S(1)} %bitcast.7, f32[35,128]{1,0:T(8,128)S(1)} %collective-permute-done.halo_ref, f32[2,128]{1,0:T(2,128)S(1)} %bitcast.8, f32[128,128]{1,0:T(8,128)S(1)} %collective-permute-done.1.main_ref, f32[35,128]{1,0:T(8,128)S(1)} %collective-permute-done.2.side_ref, ...), custom_call_target="tpu_custom_call" | custom-call | tf_op jit(solution)/shard_map/pallas_call | solution.py:289
  27.2 0.1 collective-permute-start.3
  27.3 1.2 %collective-permute-done.3 = f32[64,128]{1,0:T(8,128)S(1)} collective-permute-done((f32[64,128]{1,0:T(8,128)S(1)}, f32[64,128]{1,0:T(8,128)S(1)}, u32[]{:S(2)}, u32[]{:S(2)}) %collective-permute-start.3) | collective-permute-done | bytes 32800 | tf_op jit(solution)/shard_map/ppermute | solution.py:346
  28.5 0.7 %select_select_fusion = (f32[2,64,128]{2,1,0:T(8,128)}, f32[2,64,128]{2,1,0:T(8,128)}) fusion(f32[64,128]{1,0:T(8,128)S(1)} %collective-permute-done.3, f32[64,128]{1,0:T(8,128)S(1)} %shard_map.51, pred[2]{0:T(512)(128)(4,1)S(1)} %iota_compare_fusion, pred[]{:T(512)S(6)} %ge.3, pred[]{:T(512)S(6)} %lt.4), kind=kLoop, calls=%fused_computation | loop fusion | flops 49152 | bytes 196612 | tf_op jit(solution)/shard_map/jit(_where)/select_n | solution.py:350
  (1 shorter events, 0.0 us)
Async XLA Ops:
  0.6 16.8 %collective-permute-start.1 = (f32[128,128]{1,0:T(8,128)}, f32[128,128]{1,0:T(8,128)S(1)}, u32[]{:S(2)}, u32[]{:S(2)}) collective-permute-start(f32[128,128]{1,0:T(8,128)} %bitcast.4), channel_id=1, source_target_pairs={{8,0},{9,1},{10,2},{11,3},{12,4},{13,5},{14,6},{15,7},{0,8},{1,9},... | collective-permute-start | bytes 196616 | tf_op jit(solution)/shard_map/ppermute | solution.py:325
  3.8 13.7 %collective-permute-start = (f32[35,128]{1,0:T(8,128)S(1)}, f32[35,128]{1,0:T(8,128)S(1)}, u32[]{:S(2)}, u32[]{:S(2)}) collective-permute-start(f32[35,128]{1,0:T(8,128)S(1)} %constant_dynamic-slice_fusion), channel_id=1, source_target_pairs={{3,1},{5,3},{7,5},{9,7},{11,9},{13,11},{15,13},{19,17},{21,19},{23... | collective-permute-start | bytes 53768 | tf_op jit(solution)/shard_map/ppermute | solution.py:325
  5.9 11.5 %collective-permute-start.2 = (f32[35,128]{1,0:T(8,128)S(1)}, f32[35,128]{1,0:T(8,128)S(1)}, u32[]{:S(2)}, u32[]{:S(2)}) collective-permute-start(f32[35,128]{1,0:T(8,128)S(1)} %constant_dynamic-slice_fusion), channel_id=1, source_target_pairs={{11,1},{13,3},{15,5},{0,10},{2,12},{4,14},{3,9},{5,11},{7,13},{9,1... | collective-permute-start | bytes 53768 | tf_op jit(solution)/shard_map/ppermute | solution.py:325
  11.0 0.8 %copy-start = (f32[16384]{0:T(1024)S(1)}, f32[16384]{0:T(1024)}, u32[]{:S(2)}) copy-start(f32[16384]{0:T(1024)} %param.3) | copy-start | bytes 196612
  17.5 0.7 %copy-start.1 = (f32[256]{0:T(256)S(1)}, f32[256]{0:T(256)}, u32[]{:S(2)}) copy-start(f32[256]{0:T(256)} %param.4) | copy-start | bytes 3076
  18.1 0.7 %copy-start.2 = (s32[2]{0:T(128)S(1)}, s32[2]{0:T(128)}, u32[]{:S(2)}) copy-start(s32[2]{0:T(128)} %starts_ref.1) | copy-start | bytes 28
  27.2 1.3 %collective-permute-start.3 = (f32[64,128]{1,0:T(8,128)S(1)}, f32[64,128]{1,0:T(8,128)S(1)}, u32[]{:S(2)}, u32[]{:S(2)}) collective-permute-start(f32[64,128]{1,0:T(8,128)S(1)} %shard_map.51), channel_id=1, source_target_pairs={{0,1},{1,0},{2,3},{3,2},{4,5},{5,4},{6,7},{7,6},{8,9},{9,8},{10,11... | collective-permute-start | bytes 98312 | tf_op jit(solution)/shard_map/ppermute | solution.py:346

commit v4 on v3

--- a/solution.py
+++ b/solution.py
@@ -70,32 +70,90 @@
     return jnp.concatenate([low.astype(jnp.bfloat16), high.astype(jnp.bfloat16)], axis=0)
 
 
-def own_kernel(tiles, unroll, own_ref, z_ref, factor_ref, rows_s, center_s, shift_s, turned_s, sheet_s):
+def backwards(rows):
+    lane = lax.broadcasted_iota(jnp.int32, rows.shape, 1)
+    return jnp.take_along_axis(rows, LANES - 1 - lane, axis=1)
+
+
+def turned_back(line):
+    return pltpu.roll(jnp.broadcast_to(line, (LANES, LANES)), 0, 1, stride=1, stride_axis=0)
+
+
+def own_tile(low, high, center):
+    return jnp.concatenate([(low - center).astype(jnp.bfloat16), (high - center).astype(jnp.bfloat16)], axis=1)
+
+
+def parts(values):
+    first = values.astype(jnp.bfloat16)
+    rest = values - first.astype(jnp.float32)
+    second = rest.astype(jnp.bfloat16)
+    return first, second, (rest - second.astype(jnp.float32)).astype(jnp.bfloat16)
+
+
+def own_kernel(
+    tiles,
+    unroll,
+    starts_hbm,
+    tail_hbm,
+    own_hbm,
+    z_ref,
+    factor_ref,
+    own_ref,
+    tail_ref,
+    starts_ref,
+    rows_s,
+    back_s,
+    center_s,
+    shift_s,
+    pick_s,
+    turned_s,
+    sheet_s,
+    sem,
+):
+    copies = [
+        pltpu.make_async_copy(own_hbm, own_ref, sem.at[0]),
+        pltpu.make_async_copy(tail_hbm, tail_ref, sem.at[1]),
+        pltpu.make_async_copy(starts_hbm, starts_ref, sem.at[2]),
+    ]
+    for copy in copies:
+        copy.start()
     first_row = lax.axis_index("band") * tiles
     count = rows_s.shape[0]
+    pick_s[...] = jnp.where(lax.broadcasted_iota(jnp.int32, pick_s.shape, 0) == LANES, 1.0, 0.0)
+    center_s[...] = jnp.zeros(center_s.shape, jnp.float32)
     rows_s[pl.ds(tiles, count - tiles), :] = jnp.zeros((count - tiles, LANES), jnp.float32)
+    for copy in copies:
+        copy.wait()
     rows_s[pl.ds(0, tiles), :] = own_ref[pl.ds(first_row, tiles), :]
 
     @pl.when(first_row == 0)
     def _():
         rows_s[pl.ds(tiles, WIN), :] = own_ref[pl.ds(tiles, WIN), :]
 
-    center, spread = window_moments(rows_s[...], shift_s)
-    center_s[...] = center
+    samples = rows_s[...]
+    back_s[...] = backwards(samples)
+    center, spread = window_moments(samples, shift_s)
     factor_ref[...] = lax.rsqrt(spread + M * EPS)[:tiles]
-    ahead, _ = tile_masks()
-    first, second = (turned(rows_s[pl.ds(row, 1), :]) for row in range(2))
+    center_s[pl.ds(0, tiles), :] = center[:tiles]
+    columns = jnp.concatenate(parts(jnp.transpose(center_s[...])), axis=1)
+    _, straight = tile_masks()
+    first, second = (turned_back(back_s[pl.ds(row, 1), :]) for row in range(2))
     turned_s[...] = second
-    sheet_s[...] = sheet(first, second, ahead)
+    sheet_s[...] = sheet(second, first, straight)
 
     def group(index, _):
         line, low = turned_s[...], sheet_s[...]
-        for inner in range(unroll):
-            tile = index * unroll + inner
-            after = turned(rows_s[pl.ds(tile + 2, 1), :])
-            high = sheet(line, after, ahead)
-            z_ref[tile] = jnp.transpose(centered(low, high, center_s[pl.ds(tile, 1), :]))
-            line, low = after, high
+        for pair in range(unroll // 2):
+            tile = index * unroll + 2 * pair
+            pick = jnp.concatenate(
+                [pick_s[pl.ds(LANES - tile - t, LANES), :].astype(jnp.bfloat16) for t in range(2)], axis=1
+            )
+            spreads = jnp.dot(columns, jnp.concatenate([pick] * 3, axis=0), preferred_element_type=jnp.float32)
+            for t in range(2):
+                after = turned_back(back_s[pl.ds(tile + t + 2, 1), :])
+                high = sheet(after, line, straight)
+                z_ref[tile + t] = own_tile(low, high, spreads[:, t * LANES : (t + 1) * LANES])
+                line, low = after, high
         turned_s[...] = line
         sheet_s[...] = low
         return 0
@@ -103,27 +161,33 @@
     lax.fori_loop(0, tiles // unroll, group, 0)
 
 
-def own_side(tiles, own):
+def own_side(tiles, starts, tail, own):
     vmem = pl.BlockSpec(memory_space=pltpu.VMEM)
     count = -(-(tiles + WIN) // 8) * 8
     return pl.pallas_call(
-        functools.partial(own_kernel, tiles, UNROLL),
+        functools.partial(own_kernel, tiles, OWN_UNROLL),
         out_shape=(
             jax.ShapeDtypeStruct((tiles, LANES, M), jnp.bfloat16),
             jax.ShapeDtypeStruct((tiles, LANES), jnp.float32),
+            jax.ShapeDtypeStruct(own.shape, own.dtype),
+            jax.ShapeDtypeStruct(tail.shape, tail.dtype),
+            jax.ShapeDtypeStruct(starts.shape, starts.dtype),
         ),
-        in_specs=[vmem],
-        out_specs=(vmem, vmem),
+        in_specs=[pl.BlockSpec(memory_space=pltpu.HBM)] * 3,
+        out_specs=(vmem, vmem, vmem, vmem, pl.BlockSpec(memory_space=pltpu.SMEM)),
         scratch_shapes=[
             pltpu.VMEM((count, LANES), jnp.float32),
             pltpu.VMEM((count, LANES), jnp.float32),
+            pltpu.VMEM((LANES, LANES), jnp.float32),
             pltpu.VMEM((STEPS, count + 8, LANES), jnp.float32),
+            pltpu.VMEM((2 * LANES, LANES), jnp.float32),
             pltpu.VMEM((LANES, LANES), jnp.float32),
             pltpu.VMEM((LANES, LANES), jnp.float32),
+            pltpu.SemaphoreType.DMA((3,)),
         ],
         compiler_params=pltpu.CompilerParams(vmem_limit_bytes=VMEM_LIMIT),
         cost_estimate=pl.CostEstimate(flops=20 * tiles * LANES * M, transcendentals=0, bytes_accessed=2 * tiles * LANES * M),
-    )(own)
+    )(starts, tail, own)
 
 
 def profile_kernel(
@@ -146,7 +210,10 @@
     shift_s,
     turned_s,
     sheet_s,
-    pair_z_s,
+    even_z_s,
+    odd_z_s,
+    before_even_s,
+    before_odd_s,
     best_s,
 ):
     devices, distance, rows, tiles, role, unroll = geometry
@@ -213,12 +280,29 @@
 
     ahead, near_part = tile_masks()
 
+    half = unroll // PHASES
+
+    def prepare(first, buffer, last_ref):
+        for band in range(bands):
+            line, low = turned_s[band], sheet_s[band]
+            for inner in range(half):
+                at = first + 1 + inner
+                after = turned(shifted[band, pl.ds(at + WIN, 1), :])
+                high = sheet(line, after, ahead)
+                z = centered(low, high, center_s[band, pl.ds(at, 1), :], factor_s[band, pl.ds(at, 1), :])
+                buffer[band, inner] = z
+                line, low = after, high
+            last_ref[band] = z
+            turned_s[band] = line
+            sheet_s[band] = low
+
     for band in range(bands):
         lines = [turned(shifted[band, pl.ds(row, 1), :]) for row in range(WIN + 1)]
         sheets = [sheet(a, b, ahead) for a, b in zip(lines, lines[1:])]
         turned_s[band] = lines[-1]
         sheet_s[band] = sheets[-1]
-        pair_z_s[band] = centered(*sheets, center_s[band, pl.ds(0, 1), :], factor_s[band, pl.ds(0, 1), :])
+        before_even_s[band] = centered(*sheets, center_s[band, pl.ds(0, 1), :], factor_s[band, pl.ds(0, 1), :])
+    prepare(0, even_z_s, before_odd_s)
 
     shift = core * tiles * LANES
     low_edge = BEFORE * LANES - (position - distance) * block - shift
@@ -226,43 +310,45 @@
     lo = jnp.where(is_col, low_edge, 0)
     hi = jnp.where(is_col, 1 << 30, high_edge)
 
-    lines = [turned(late_s[pl.ds(row, 1), :]) for row in range(2 * WIN)]
-    sheets = [sheet(a, b, ahead) for a, b in zip(lines, lines[1:])]
+    back = backwards(late_s[...])
+    lines = [turned_back(back[row : row + 1]) for row in range(2 * WIN)]
+    sheets = [sheet(b, a, near_part) for a, b in zip(lines, lines[1:])]
     for tile in range(WIN):
-        late_z_s[tile] = jnp.transpose(centered(sheets[tile], sheets[tile + 1], late_center[tile : tile + 1]))
-
-    def steps(masked, group, _):
-        lines = [turned_s[band] for band in range(bands)]
-        sheets = [sheet_s[band] for band in range(bands)]
-        pairs = [pair_z_s[band] for band in range(bands)]
-        for inner in range(unroll):
-            tile = group * unroll + inner
+        spread_out = jnp.transpose(jnp.broadcast_to(late_center[tile : tile + 1], (LANES, LANES)))
+        late_z_s[tile] = own_tile(sheets[tile], sheets[tile + 1], spread_out)
+
+    def products(masked, group, phase, before, buffer):
+        first = group * unroll + phase * half
+        for inner in range(half):
+            tile = first + inner
             own = z_ref[tile]
-            if inner >= unroll - WIN:
-                own = jnp.where(group == groups - 1, late_z_s[inner + WIN - unroll], own)
+            tile_in_group = phase * half + inner
+            late = tile_in_group - (unroll - WIN)
+            if late >= 0:
+                own = jnp.where(group == groups - 1, late_z_s[late], own)
             best = None
             for band in range(bands):
-                at = tile + 1
-                line = turned(shifted[band, pl.ds(at + WIN, 1), :])
-                high = sheet(lines[band], line, ahead)
-                following = centered(
-                    sheets[band], high, center_s[band, pl.ds(at, 1), :], factor_s[band, pl.ds(at, 1), :]
-                )
-                lines[band], sheets[band] = line, high
-                both = jnp.concatenate([pairs[band], following], axis=1)
-                pairs[band] = following
+                here = before[band] if inner == 0 else buffer[band, inner - 1]
+                both = jnp.concatenate([here, buffer[band, inner]], axis=1)
                 scores = jnp.dot(own, both, preferred_element_type=jnp.float32)
                 if masked:
                     index = begins[band] + tile * LANES + lax.broadcasted_iota(jnp.int32, (1, 2 * LANES), 1)
                     scores = jnp.where((index >= lo) & (index < hi), scores, -1e30)
                 mixed = jnp.where(near_part, scores[:, :LANES], scores[:, LANES:])
                 best = mixed if best is None else jnp.maximum(best, mixed)
-            found = jnp.max(best, axis=1, keepdims=True)
-            best_s[...] = jnp.where(lane == tile, found, best_s[...])
-        for band in range(bands):
-            turned_s[band] = lines[band]
-            sheet_s[band] = sheets[band]
-            pair_z_s[band] = pairs[band]
+            best_s[tile] = best
+
+    def steps(masked, group, _):
+        first = group * unroll
+        for phase in range(PHASES):
+            before, buffer, other, other_buffer = (
+                (before_even_s, even_z_s, before_odd_s, odd_z_s)
+                if phase % 2 == 0
+                else (before_odd_s, odd_z_s, before_even_s, even_z_s)
+            )
+            at = first + phase * half
+            products(masked, group, phase, before, buffer)
+            prepare(at + half, other_buffer, before)
         return 0
 
     size = unroll * LANES
@@ -275,7 +361,15 @@
     lax.fori_loop(0, first_full, functools.partial(steps, True), 0)
     lax.fori_loop(first_full, last_full, functools.partial(steps, False), 0)
     lax.fori_loop(last_full, groups, functools.partial(steps, True), 0)
-    found = jnp.transpose(best_s[...])[:tiles]
+
+    def reduce(group, columns):
+        for inner in range(unroll):
+            tile = group * unroll + inner
+            columns = jnp.where(lane == tile, jnp.max(best_s[tile], axis=1, keepdims=True), columns)
+        return columns
+
+    columns = lax.fori_loop(0, groups, reduce, jnp.zeros((LANES, LANES), jnp.float32))
+    found = jnp.transpose(columns)[:tiles]
     out_ref[...] = jnp.maximum(found * factor_ref[...], -1.0)
     late = jnp.maximum(found[early:] * late_factor[:WIN], -1.0)
     out_ref[pl.ds(early, WIN), :] = late
@@ -285,7 +379,7 @@
     devices, distance, rows, tiles, role = geometry
     bands = starts.shape[0]
     vmem = pl.BlockSpec(memory_space=pltpu.VMEM)
-    pad = -(-(tiles + 2 + WIN) // 8) * 8
+    pad = -(-(tiles + UNROLL // PHASES + 1 + WIN) // 8) * 8
     return pl.pallas_call(
         functools.partial(profile_kernel, geometry + (UNROLL,)),
         out_shape=jax.ShapeDtypeStruct((tiles, LANES), jnp.float32),
@@ -301,8 +395,11 @@
             pltpu.VMEM((STEPS, bands * pad + 8, LANES), jnp.float32),
             pltpu.VMEM((bands, LANES, LANES), jnp.float32),
             pltpu.VMEM((bands, LANES, LANES), jnp.float32),
+            pltpu.VMEM((bands, UNROLL // PHASES, M, LANES), jnp.bfloat16),
+            pltpu.VMEM((bands, UNROLL // PHASES, M, LANES), jnp.bfloat16),
             pltpu.VMEM((bands, M, LANES), jnp.bfloat16),
-            pltpu.VMEM((LANES, LANES), jnp.float32),
+            pltpu.VMEM((bands, M, LANES), jnp.bfloat16),
+            pltpu.VMEM((tiles, LANES, LANES), jnp.float32),
         ],
         compiler_params=pltpu.CompilerParams(vmem_limit_bytes=VMEM_LIMIT),
     )(starts, own, halo, tail, main, side, factor, z)
@@ -339,10 +436,11 @@
     edge = lax.dynamic_slice_in_dim(own, jnp.where(core == 0, rows - AFTER, 0), AFTER)
     sides = [move(edge, pairs) for _, _, pairs in roles]
     halo = move(edge, [(d, 1, 1) for d in range(devices)])
-    z, factor = own_side(tiles, own)
+    in_hbm = [pltpu.with_memory_space_constraint(value, pltpu.HBM) for value in (band_starts, tail, own)]
+    z, factor, own, tail, starts = own_side(tiles, *in_hbm)
     found = []
     for (role, _, _), main, side in zip(roles, mains, sides):
-        part = profile((devices, distance, rows, tiles, role), band_starts, own, halo, tail, main, side, factor, z)
+        part = profile((devices, distance, rows, tiles, role), starts, own, halo, tail, main, side, factor, z)
         other = lax.ppermute(part, "band", [(0, 1), (1, 0)])
         mine = jnp.arange(cores)[:, None, None] == core
         found.append(jnp.where(mine, part[None], other[None]).reshape(-1))
@@ -351,7 +449,9 @@
     return row_best, col_best
 
 
-UNROLL = 8
+UNROLL = 16
+OWN_UNROLL = 8
+PHASES = 8
 VMEM_LIMIT = 24 << 20
 
 

time: 29.5 us -> 24.7 us (0.84)
  the two profiles are of different devices: /device:TPU:5 before, /device:TPU:7 now
where the time goes in v4:
time: 24.7 us; the launch traced here: 24.5 us
  Pallas kernels  11.4 us (46%)
  starting transfers between devices  9.63 us (39%)
  waiting for transfers between devices  1.18 us (5%)
  local copies, waits for them, and re-layouts  0.78 us (3%)
  other arithmetic  0.74 us (3%)
  between operations  0.71 us (3%)
    ppermute x3, starting transfers between devices, move(): return lax.ppermute(value, ('tm', 'band'), route)  9.56 us
    pallas_call x1, Pallas kernels, profile(): pl.pallas_call(functools.partial(profile_kernel, geometry + (UNROLL,)), o...  6.81 us
    pallas_call x1, Pallas kernels, own_side(): pl.pallas_call(functools.partial(own_kernel, tiles, OWN_UNROLL), out_shap...  4.62 us
    ppermute x1, waiting for transfers between devices, body(): other = lax.ppermute(part, 'band', [(0, 1), (1, 0)])  1.17 us
    dynamic_slice x1, local copies, waits for them, and re-layouts, body(): lax.dynamic_slice_in_dim(own, jnp.where(core == 0, rows - AFTER, 0), AFTER)  0.78 us
    select_n x1, other arithmetic, body(): col_best = jnp.where(position >= distance, found[-1], -1.0)  0.73 us
  transfers between devices with their start and end apart: 4, of which 1 were waited for; matrix products, arithmetic and copies ran while one was open for 3% of the time, Pallas kernels for 19%

profile of v4, /device:TPU:7, one launch (start us, length us, event | category | flops | bytes accessed | tf_op | source)
XLA Modules:
  0.0 24.5 jit_solution(14846881699734443809)
XLA Ops:
  0.6 2.4 %collective-permute-start.1 = (f32[128,128]{1,0:T(8,128)}, f32[128,128]{1,0:T(8,128)S(1)}, u32[]{:S(2)}, u32[]{:S(2)}) collective-permute-start(f32[128,128]{1,0:T(8,128)} %bitcast.6), channel_id=1, source_target_pairs={{8,0},{9,1},{10,2},{11,3},{12,4},{13,5},{14,6},{15,7},{0,8},{1,9},... | collective-permute-start | bytes 196616 | tf_op jit(solution)/shard_map/ppermute | solution.py:422
  3.0 0.8 %constant_dynamic-slice_fusion = f32[35,128]{1,0:T(8,128)S(1)} fusion(f32[128,128]{1,0:T(8,128)} %bitcast.7, s32[]{:T(128)S(6)} %select_n.32), kind=kLoop, calls=%fused_computation.3 | loop fusion | bytes 35844 | tf_op jit(solution)/shard_map/dynamic_slice | solution.py:436
  3.8 2.1 %collective-permute-start = (f32[35,128]{1,0:T(8,128)S(1)}, f32[35,128]{1,0:T(8,128)S(1)}, u32[]{:S(2)}, u32[]{:S(2)}) collective-permute-start(f32[35,128]{1,0:T(8,128)S(1)} %constant_dynamic-slice_fusion), channel_id=1, source_target_pairs={{3,1},{5,3},{7,5},{9,7},{11,9},{13,11},{15,13},{19,17},{21,19},{23... | collective-permute-start | bytes 53768 | tf_op jit(solution)/shard_map/ppermute | solution.py:422
  5.9 5.1 %collective-permute-start.2 = (f32[35,128]{1,0:T(8,128)S(1)}, f32[35,128]{1,0:T(8,128)S(1)}, u32[]{:S(2)}, u32[]{:S(2)}) collective-permute-start(f32[35,128]{1,0:T(8,128)S(1)} %constant_dynamic-slice_fusion), channel_id=1, source_target_pairs={{11,1},{13,3},{15,5},{0,10},{2,12},{4,14},{3,9},{5,11},{7,13},{9,1... | collective-permute-start | bytes 53768 | tf_op jit(solution)/shard_map/ppermute | solution.py:422
  11.0 4.6 %shard_map.50 = (bf16[64,128,256]{2,1,0:T(8,128)(2,1)S(1)}, f32[64,128]{1,0:T(8,128)S(1)}, f32[128,128]{1,0:T(8,128)S(1)}, f32[2,128]{1,0:T(2,128)S(1)}, s32[2]{0:T(128)S(1)}) custom-call(s32[2]{0:T(128)} %starts_hbm.1, f32[2,128]{1,0:T(2,128)} %bitcast.9, f32[128,128]{1,0:T(8,128)} %bitcast.8), custom_call_target="tpu_custom_call" | custom-call | flops 41943040 | bytes 4194304 | tf_op jit(solution)/shard_map/pallas_call | solution.py:167
  15.6 0.0 collective-permute-done.halo_ref
  15.6 0.0 collective-permute-done.2.side_ref
  15.6 0.0 collective-permute-done.1.main_ref
  15.6 6.8 %shard_map.51 = f32[64,128]{1,0:T(8,128)S(1)} custom-call(s32[2]{0:T(128)S(1)} %get-tuple-element.7.starts_ref, f32[128,128]{1,0:T(8,128)S(1)} %get-tuple-element.8.own_ref, f32[35,128]{1,0:T(8,128)S(1)} %collective-permute-done.halo_ref, f32[2,128]{1,0:T(2,128)S(1)} %get-tuple-element.9.tail_ref, f32[128,128]{1,0:T(8,128)S(1)} %collective-permute-done.1.main_ref, ...), custom_call_target="tpu_custom_call" | custom-call | tf_op jit(solution)/shard_map/pallas_call | solution.py:383
  22.5 0.1 collective-permute-start.3
  22.6 1.2 %collective-permute-done.3 = f32[64,128]{1,0:T(8,128)S(1)} collective-permute-done((f32[64,128]{1,0:T(8,128)S(1)}, f32[64,128]{1,0:T(8,128)S(1)}, u32[]{:S(2)}, u32[]{:S(2)}) %collective-permute-start.3) | collective-permute-done | bytes 32800 | tf_op jit(solution)/shard_map/ppermute | solution.py:444
  23.7 0.7 %select_select_fusion = (f32[2,64,128]{2,1,0:T(8,128)}, f32[2,64,128]{2,1,0:T(8,128)}) fusion(f32[64,128]{1,0:T(8,128)S(1)} %collective-permute-done.3, f32[64,128]{1,0:T(8,128)S(1)} %shard_map.51, pred[2]{0:T(512)(128)(4,1)S(1)} %iota_compare_fusion, pred[]{:T(512)S(6)} %ge.3, pred[]{:T(512)S(6)} %lt.4), kind=kLoop, calls=%fused_computation | loop fusion | flops 49152 | bytes 196612 | tf_op jit(solution)/shard_map/jit(_where)/select_n | solution.py:448
  (1 shorter events, 0.0 us)
Async XLA Ops:
  0.6 15.0 %collective-permute-start.1 = (f32[128,128]{1,0:T(8,128)}, f32[128,128]{1,0:T(8,128)S(1)}, u32[]{:S(2)}, u32[]{:S(2)}) collective-permute-start(f32[128,128]{1,0:T(8,128)} %bitcast.6), channel_id=1, source_target_pairs={{8,0},{9,1},{10,2},{11,3},{12,4},{13,5},{14,6},{15,7},{0,8},{1,9},... | collective-permute-start | bytes 196616 | tf_op jit(solution)/shard_map/ppermute | solution.py:422
  3.8 11.8 %collective-permute-start = (f32[35,128]{1,0:T(8,128)S(1)}, f32[35,128]{1,0:T(8,128)S(1)}, u32[]{:S(2)}, u32[]{:S(2)}) collective-permute-start(f32[35,128]{1,0:T(8,128)S(1)} %constant_dynamic-slice_fusion), channel_id=1, source_target_pairs={{3,1},{5,3},{7,5},{9,7},{11,9},{13,11},{15,13},{19,17},{21,19},{23... | collective-permute-start | bytes 53768 | tf_op jit(solution)/shard_map/ppermute | solution.py:422
  5.9 9.7 %collective-permute-start.2 = (f32[35,128]{1,0:T(8,128)S(1)}, f32[35,128]{1,0:T(8,128)S(1)}, u32[]{:S(2)}, u32[]{:S(2)}) collective-permute-start(f32[35,128]{1,0:T(8,128)S(1)} %constant_dynamic-slice_fusion), channel_id=1, source_target_pairs={{11,1},{13,3},{15,5},{0,10},{2,12},{4,14},{3,9},{5,11},{7,13},{9,1... | collective-permute-start | bytes 53768 | tf_op jit(solution)/shard_map/ppermute | solution.py:422
  22.5 1.3 %collective-permute-start.3 = (f32[64,128]{1,0:T(8,128)S(1)}, f32[64,128]{1,0:T(8,128)S(1)}, u32[]{:S(2)}, u32[]{:S(2)}) collective-permute-start(f32[64,128]{1,0:T(8,128)S(1)} %shard_map.51), channel_id=1, source_target_pairs={{0,1},{1,0},{2,3},{3,2},{4,5},{5,4},{6,7},{7,6},{8,9},{9,8},{10,11... | collective-permute-start | bytes 98312 | tf_op jit(solution)/shard_map/ppermute | solution.py:444

commit v5 on v4

--- a/solution.py
+++ b/solution.py
@@ -6,6 +6,7 @@
 from jax.experimental import pallas as pl
 from jax.experimental.pallas import tpu as pltpu
 from jax.sharding import PartitionSpec as P
+
 
 M = 256
 LANES = 128
@@ -165,7 +166,7 @@
     vmem = pl.BlockSpec(memory_space=pltpu.VMEM)
     count = -(-(tiles + WIN) // 8) * 8
     return pl.pallas_call(
-        functools.partial(own_kernel, tiles, OWN_UNROLL),
+        functools.partial(own_kernel, tiles, min(tiles, OWN_UNROLL)),
         out_shape=(
             jax.ShapeDtypeStruct((tiles, LANES, M), jnp.bfloat16),
             jax.ShapeDtypeStruct((tiles, LANES), jnp.float32),
@@ -236,7 +237,7 @@
     @pl.when(jnp.logical_not(is_col) & (core != 0))
     def _():
         pair_s[pl.ds(0, tiles), :] = main_ref[pl.ds(rows - tiles, tiles), :]
-        pair_s[pl.ds(tiles, AFTER), :] = side_ref[...]
+        pair_s[pl.ds(tiles, AFTER), :] = side_ref[pl.ds(0, AFTER), :]
 
         @pl.when(position == devices - distance - 1)
         def _():
@@ -244,7 +245,7 @@
 
     @pl.when(is_col & (core == 0))
     def _():
-        pair_s[pl.ds(0, BEFORE), :] = side_ref[pl.ds(WIN, BEFORE), :]
+        pair_s[pl.ds(0, BEFORE), :] = side_ref[pl.ds(rows - BEFORE, BEFORE), :]
         pair_s[pl.ds(BEFORE, tiles + WIN), :] = main_ref[pl.ds(0, tiles + WIN), :]
 
     @pl.when(is_col & (core != 0))
@@ -341,7 +342,7 @@
     def steps(masked, group, _):
         first = group * unroll
         for phase in range(PHASES):
-            before, buffer, other, other_buffer = (
+            before, buffer, _, other_buffer = (
                 (before_even_s, even_z_s, before_odd_s, odd_z_s)
                 if phase % 2 == 0
                 else (before_odd_s, odd_z_s, before_even_s, even_z_s)
@@ -376,7 +377,7 @@
 
 
 def profile(geometry, starts, own, halo, tail, main, side, factor, z):
-    devices, distance, rows, tiles, role = geometry
+    _, _, _, tiles, _ = geometry
     bands = starts.shape[0]
     vmem = pl.BlockSpec(memory_space=pltpu.VMEM)
     pad = -(-(tiles + UNROLL // PHASES + 1 + WIN) // 8) * 8
@@ -432,10 +433,9 @@
         (False, main_row, side_row),
         (True, main_col, side_col),
     ]
+    halo = move(own, [(d, 1, 1) for d in range(devices)])
+    sides = [move(own, pairs) for _, _, pairs in roles]
     mains = [move(own, pairs) for _, pairs, _ in roles]
-    edge = lax.dynamic_slice_in_dim(own, jnp.where(core == 0, rows - AFTER, 0), AFTER)
-    sides = [move(edge, pairs) for _, _, pairs in roles]
-    halo = move(edge, [(d, 1, 1) for d in range(devices)])
     in_hbm = [pltpu.with_memory_space_constraint(value, pltpu.HBM) for value in (band_starts, tail, own)]
     z, factor, own, tail, starts = own_side(tiles, *in_hbm)
     found = []
@@ -450,7 +450,7 @@
 
 
 UNROLL = 16
-OWN_UNROLL = 8
+OWN_UNROLL = 64
 PHASES = 8
 VMEM_LIMIT = 24 << 20
 

time: 24.7 us -> 23 us (0.931)
  the two profiles are of different devices: /device:TPU:7 before, /device:TPU:0 now
where the time goes in v5:
time: 23 us; the launch traced here: 22.8 us
  Pallas kernels  10.4 us (45%)
  starting transfers between devices  10.1 us (44%)
  waiting for transfers between devices  0.86 us (4%)
  other arithmetic  0.74 us (3%)
  between operations  0.69 us (3%)
    ppermute x3, starting transfers between devices, move(): return lax.ppermute(value, ('tm', 'band'), route)  7.98 us
    pallas_call x1, Pallas kernels, profile(): pl.pallas_call(functools.partial(profile_kernel, geometry + (UNROLL,)), o...  6.81 us
    pallas_call x1, Pallas kernels, own_side(): pl.pallas_call(functools.partial(own_kernel, tiles, min(tiles, OWN_UNROLL...  3.64 us
    ppermute x1, starting transfers between devices, body(): other = lax.ppermute(part, 'band', [(0, 1), (1, 0)])  2.11 us
    ppermute x1, waiting for transfers between devices, body(): other = lax.ppermute(part, 'band', [(0, 1), (1, 0)])  0.85 us
    select_n x1, other arithmetic, body(): col_best = jnp.where(position >= distance, found[-1], -1.0)  0.73 us
  transfers between devices with their start and end apart: 4, of which 1 were waited for; matrix products, arithmetic and copies ran while one was open for 0% of the time, Pallas kernels for 16%

profile of v5, /device:TPU:0, one launch (start us, length us, event | category | flops | bytes accessed | tf_op | source)
XLA Modules:
  0.0 22.8 jit_solution(1524233178205524663)
XLA Ops:
  0.6 0.7 %collective-permute-start = (f32[128,128]{1,0:T(8,128)}, f32[128,128]{1,0:T(8,128)S(1)}, u32[]{:S(2)}, u32[]{:S(2)}) collective-permute-start(f32[128,128]{1,0:T(8,128)} %bitcast.6), channel_id=1, source_target_pairs={{3,1},{5,3},{7,5},{9,7},{11,9},{13,11},{15,13},{19,17},{21,19},{23... | collective-permute-start | bytes 196616 | tf_op jit(solution)/shard_map/ppermute | solution.py:423
  1.3 4.1 %collective-permute-start.1 = (f32[128,128]{1,0:T(8,128)}, f32[128,128]{1,0:T(8,128)S(1)}, u32[]{:S(2)}, u32[]{:S(2)}) collective-permute-start(f32[128,128]{1,0:T(8,128)} %bitcast.7), channel_id=1, source_target_pairs={{8,0},{9,1},{10,2},{11,3},{12,4},{13,5},{14,6},{15,7},{0,8},{1,9},... | collective-permute-start | bytes 196616 | tf_op jit(solution)/shard_map/ppermute | solution.py:423
  5.4 3.2 %collective-permute-start.2 = (f32[128,128]{1,0:T(8,128)}, f32[128,128]{1,0:T(8,128)S(1)}, u32[]{:S(2)}, u32[]{:S(2)}) collective-permute-start(f32[128,128]{1,0:T(8,128)} %bitcast.8), channel_id=1, source_target_pairs={{11,1},{13,3},{15,5},{0,10},{2,12},{4,14},{3,9},{5,11},{7,13},{9,1... | collective-permute-start | bytes 196616 | tf_op jit(solution)/shard_map/ppermute | solution.py:423
  8.6 3.6 %shard_map.50 = (bf16[64,128,256]{2,1,0:T(8,128)(2,1)S(1)}, f32[64,128]{1,0:T(8,128)S(1)}, f32[128,128]{1,0:T(8,128)S(1)}, f32[2,128]{1,0:T(2,128)S(1)}, s32[2]{0:T(128)S(1)}) custom-call(s32[2]{0:T(128)} %starts_hbm.1, f32[2,128]{1,0:T(2,128)} %bitcast.10, f32[128,128]{1,0:T(8,128)} %bitcast.9), custom_call_target="tpu_custom_call" | custom-call | flops 41943040 | bytes 4194304 | tf_op jit(solution)/shard_map/pallas_call | solution.py:168
  12.3 0.0 collective-permute-done.halo_ref
  12.3 0.0 collective-permute-done.1.main_ref
  12.3 0.0 collective-permute-done.2.side_ref
  12.3 6.8 %shard_map.51 = f32[64,128]{1,0:T(8,128)S(1)} custom-call(s32[2]{0:T(128)S(1)} %get-tuple-element.7.starts_ref, f32[128,128]{1,0:T(8,128)S(1)} %get-tuple-element.8.own_ref, f32[128,128]{1,0:T(8,128)S(1)} %collective-permute-done.halo_ref, f32[2,128]{1,0:T(2,128)S(1)} %get-tuple-element.9.tail_ref, f32[128,128]{1,0:T(8,128)S(1)} %collective-permute-done.1.main_ref, ...), custom_call_target="tpu_custom_call" | custom-call | tf_op jit(solution)/shard_map/pallas_call | solution.py:384
  19.1 2.1 %collective-permute-start.3 = (f32[64,128]{1,0:T(8,128)S(1)}, f32[64,128]{1,0:T(8,128)S(1)}, u32[]{:S(2)}, u32[]{:S(2)}) collective-permute-start(f32[64,128]{1,0:T(8,128)S(1)} %shard_map.51), channel_id=1, source_target_pairs={{0,1},{1,0},{2,3},{3,2},{4,5},{5,4},{6,7},{7,6},{8,9},{9,8},{10,11... | collective-permute-start | bytes 98312 | tf_op jit(solution)/shard_map/ppermute | solution.py:444
  21.2 0.9 %collective-permute-done.3 = f32[64,128]{1,0:T(8,128)S(1)} collective-permute-done((f32[64,128]{1,0:T(8,128)S(1)}, f32[64,128]{1,0:T(8,128)S(1)}, u32[]{:S(2)}, u32[]{:S(2)}) %collective-permute-start.3) | collective-permute-done | bytes 32800 | tf_op jit(solution)/shard_map/ppermute | solution.py:444
  22.1 0.7 %select_select_fusion = (f32[2,64,128]{2,1,0:T(8,128)}, f32[2,64,128]{2,1,0:T(8,128)}) fusion(f32[64,128]{1,0:T(8,128)S(1)} %collective-permute-done.3, f32[64,128]{1,0:T(8,128)S(1)} %shard_map.51, pred[2]{0:T(512)(128)(4,1)S(1)} %iota_compare_fusion, pred[]{:T(512)S(6)} %ge.3, pred[]{:T(512)S(6)} %lt.3), kind=kLoop, calls=%fused_computation | loop fusion | flops 49152 | bytes 196612 | tf_op jit(solution)/shard_map/jit(_where)/select_n | solution.py:448
  (1 shorter events, 0.0 us)
Async XLA Ops:
  0.6 11.7 %collective-permute-start = (f32[128,128]{1,0:T(8,128)}, f32[128,128]{1,0:T(8,128)S(1)}, u32[]{:S(2)}, u32[]{:S(2)}) collective-permute-start(f32[128,128]{1,0:T(8,128)} %bitcast.6), channel_id=1, source_target_pairs={{3,1},{5,3},{7,5},{9,7},{11,9},{13,11},{15,13},{19,17},{21,19},{23... | collective-permute-start | bytes 196616 | tf_op jit(solution)/shard_map/ppermute | solution.py:423
  1.3 11.0 %collective-permute-start.1 = (f32[128,128]{1,0:T(8,128)}, f32[128,128]{1,0:T(8,128)S(1)}, u32[]{:S(2)}, u32[]{:S(2)}) collective-permute-start(f32[128,128]{1,0:T(8,128)} %bitcast.7), channel_id=1, source_target_pairs={{8,0},{9,1},{10,2},{11,3},{12,4},{13,5},{14,6},{15,7},{0,8},{1,9},... | collective-permute-start | bytes 196616 | tf_op jit(solution)/shard_map/ppermute | solution.py:423
  5.4 6.9 %collective-permute-start.2 = (f32[128,128]{1,0:T(8,128)}, f32[128,128]{1,0:T(8,128)S(1)}, u32[]{:S(2)}, u32[]{:S(2)}) collective-permute-start(f32[128,128]{1,0:T(8,128)} %bitcast.8), channel_id=1, source_target_pairs={{11,1},{13,3},{15,5},{0,10},{2,12},{4,14},{3,9},{5,11},{7,13},{9,1... | collective-permute-start | bytes 196616 | tf_op jit(solution)/shard_map/ppermute | solution.py:423
  19.1 3.0 %collective-permute-start.3 = (f32[64,128]{1,0:T(8,128)S(1)}, f32[64,128]{1,0:T(8,128)S(1)}, u32[]{:S(2)}, u32[]{:S(2)}) collective-permute-start(f32[64,128]{1,0:T(8,128)S(1)} %shard_map.51), channel_id=1, source_target_pairs={{0,1},{1,0},{2,3},{3,2},{4,5},{5,4},{6,7},{7,6},{8,9},{9,8},{10,11... | collective-permute-start | bytes 98312 | tf_op jit(solution)/shard_map/ppermute | solution.py:444

commit v6 on v5

--- a/solution.py
+++ b/solution.py
@@ -339,7 +339,7 @@
                 best = mixed if best is None else jnp.maximum(best, mixed)
             best_s[tile] = best
 
-    def steps(masked, group, _):
+    def steps(masked, group):
         first = group * unroll
         for phase in range(PHASES):
             before, buffer, _, other_buffer = (
@@ -359,17 +359,31 @@
         last_full = jnp.minimum(last_full, (hi - begin - LANES) // size)
     first_full = jnp.clip(first_full, 0, groups)
     last_full = jnp.clip(last_full, first_full, groups)
-    lax.fori_loop(0, first_full, functools.partial(steps, True), 0)
-    lax.fori_loop(first_full, last_full, functools.partial(steps, False), 0)
-    lax.fori_loop(last_full, groups, functools.partial(steps, True), 0)
+
+    def either(group, _):
+        full = (group >= first_full) & (group < last_full)
+
+        @pl.when(full)
+        def _():
+            steps(False, group)
+
+        @pl.when(jnp.logical_not(full))
+        def _():
+            steps(True, group)
+
+        return 0
+
+    lax.fori_loop(0, groups, either, 0)
+
+    together = min(tiles, REDUCE)
 
     def reduce(group, columns):
-        for inner in range(unroll):
-            tile = group * unroll + inner
+        for inner in range(together):
+            tile = group * together + inner
             columns = jnp.where(lane == tile, jnp.max(best_s[tile], axis=1, keepdims=True), columns)
         return columns
 
-    columns = lax.fori_loop(0, groups, reduce, jnp.zeros((LANES, LANES), jnp.float32))
+    columns = lax.fori_loop(0, tiles // together, reduce, jnp.zeros((LANES, LANES), jnp.float32))
     found = jnp.transpose(columns)[:tiles]
     out_ref[...] = jnp.maximum(found * factor_ref[...], -1.0)
     late = jnp.maximum(found[early:] * late_factor[:WIN], -1.0)
@@ -449,9 +463,10 @@
     return row_best, col_best
 
 
-UNROLL = 16
+UNROLL = 32
 OWN_UNROLL = 64
-PHASES = 8
+PHASES = 16
+REDUCE = 64
 VMEM_LIMIT = 24 << 20
 
 

time: 23 us -> 22.5 us (0.978)
  Pallas kernels: 10.4 us -> 9.9 us
    pallas_call x1, Pallas kernels: 6.81 us -> 6.25 us  [profile(): pl.pallas_call(functools.partial(profile_kernel, geometry + (UNROLL,)), o...]
where the time goes in v6:
time: 22.5 us; the launch traced here: 22.3 us
  starting transfers between devices  10.1 us (45%)
  Pallas kernels  9.9 us (44%)
  waiting for transfers between devices  0.86 us (4%)
  other arithmetic  0.74 us (3%)
  between operations  0.69 us (3%)
    ppermute x3, starting transfers between devices, move(): return lax.ppermute(value, ('tm', 'band'), route)  7.98 us
    pallas_call x1, Pallas kernels, profile(): pl.pallas_call(functools.partial(profile_kernel, geometry + (UNROLL,)), o...  6.25 us
    pallas_call x1, Pallas kernels, own_side(): pl.pallas_call(functools.partial(own_kernel, tiles, min(tiles, OWN_UNROLL...  3.64 us
    ppermute x1, starting transfers between devices, body(): other = lax.ppermute(part, 'band', [(0, 1), (1, 0)])  2.12 us
    ppermute x1, waiting for transfers between devices, body(): other = lax.ppermute(part, 'band', [(0, 1), (1, 0)])  0.85 us
    select_n x1, other arithmetic, body(): col_best = jnp.where(position >= distance, found[-1], -1.0)  0.73 us
  transfers between devices with their start and end apart: 4, of which 1 were waited for; matrix products, arithmetic and copies ran while one was open for 0% of the time, Pallas kernels for 16%

profile of v6, /device:TPU:0, one launch (start us, length us, event | category | flops | bytes accessed | tf_op | source)
XLA Modules:
  0.0 22.3 jit_solution(11537785408694701281)
XLA Ops:
  0.6 0.7 %collective-permute-start = (f32[128,128]{1,0:T(8,128)}, f32[128,128]{1,0:T(8,128)S(1)}, u32[]{:S(2)}, u32[]{:S(2)}) collective-permute-start(f32[128,128]{1,0:T(8,128)} %bitcast.6), channel_id=1, source_target_pairs={{3,1},{5,3},{7,5},{9,7},{11,9},{13,11},{15,13},{19,17},{21,19},{23... | collective-permute-start | bytes 196616 | tf_op jit(solution)/shard_map/ppermute | solution.py:437
  1.3 4.1 %collective-permute-start.1 = (f32[128,128]{1,0:T(8,128)}, f32[128,128]{1,0:T(8,128)S(1)}, u32[]{:S(2)}, u32[]{:S(2)}) collective-permute-start(f32[128,128]{1,0:T(8,128)} %bitcast.7), channel_id=1, source_target_pairs={{8,0},{9,1},{10,2},{11,3},{12,4},{13,5},{14,6},{15,7},{0,8},{1,9},... | collective-permute-start | bytes 196616 | tf_op jit(solution)/shard_map/ppermute | solution.py:437
  5.4 3.2 %collective-permute-start.2 = (f32[128,128]{1,0:T(8,128)}, f32[128,128]{1,0:T(8,128)S(1)}, u32[]{:S(2)}, u32[]{:S(2)}) collective-permute-start(f32[128,128]{1,0:T(8,128)} %bitcast.8), channel_id=1, source_target_pairs={{11,1},{13,3},{15,5},{0,10},{2,12},{4,14},{3,9},{5,11},{7,13},{9,1... | collective-permute-start | bytes 196616 | tf_op jit(solution)/shard_map/ppermute | solution.py:437
  8.6 3.6 %shard_map.50 = (bf16[64,128,256]{2,1,0:T(8,128)(2,1)S(1)}, f32[64,128]{1,0:T(8,128)S(1)}, f32[128,128]{1,0:T(8,128)S(1)}, f32[2,128]{1,0:T(2,128)S(1)}, s32[2]{0:T(128)S(1)}) custom-call(s32[2]{0:T(128)} %starts_hbm.1, f32[2,128]{1,0:T(2,128)} %bitcast.10, f32[128,128]{1,0:T(8,128)} %bitcast.9), custom_call_target="tpu_custom_call" | custom-call | flops 41943040 | bytes 4194304 | tf_op jit(solution)/shard_map/pallas_call | solution.py:168
  12.3 0.0 collective-permute-done.halo_ref
  12.3 0.0 collective-permute-done.1.main_ref
  12.3 0.0 collective-permute-done.2.side_ref
  12.3 6.3 %shard_map.51 = f32[64,128]{1,0:T(8,128)S(1)} custom-call(s32[2]{0:T(128)S(1)} %get-tuple-element.7.starts_ref, f32[128,128]{1,0:T(8,128)S(1)} %get-tuple-element.8.own_ref, f32[128,128]{1,0:T(8,128)S(1)} %collective-permute-done.halo_ref, f32[2,128]{1,0:T(2,128)S(1)} %get-tuple-element.9.tail_ref, f32[128,128]{1,0:T(8,128)S(1)} %collective-permute-done.1.main_ref, ...), custom_call_target="tpu_custom_call" | custom-call | tf_op jit(solution)/shard_map/pallas_call | solution.py:398
  18.6 2.1 %collective-permute-start.3 = (f32[64,128]{1,0:T(8,128)S(1)}, f32[64,128]{1,0:T(8,128)S(1)}, u32[]{:S(2)}, u32[]{:S(2)}) collective-permute-start(f32[64,128]{1,0:T(8,128)S(1)} %shard_map.51), channel_id=1, source_target_pairs={{0,1},{1,0},{2,3},{3,2},{4,5},{5,4},{6,7},{7,6},{8,9},{9,8},{10,11... | collective-permute-start | bytes 98312 | tf_op jit(solution)/shard_map/ppermute | solution.py:458
  20.7 0.9 %collective-permute-done.3 = f32[64,128]{1,0:T(8,128)S(1)} collective-permute-done((f32[64,128]{1,0:T(8,128)S(1)}, f32[64,128]{1,0:T(8,128)S(1)}, u32[]{:S(2)}, u32[]{:S(2)}) %collective-permute-start.3) | collective-permute-done | bytes 32800 | tf_op jit(solution)/shard_map/ppermute | solution.py:458
  21.6 0.7 %select_select_fusion = (f32[2,64,128]{2,1,0:T(8,128)}, f32[2,64,128]{2,1,0:T(8,128)}) fusion(f32[64,128]{1,0:T(8,128)S(1)} %collective-permute-done.3, f32[64,128]{1,0:T(8,128)S(1)} %shard_map.51, pred[2]{0:T(512)(128)(4,1)S(1)} %iota_compare_fusion, pred[]{:T(512)S(6)} %ge.3, pred[]{:T(512)S(6)} %lt.3), kind=kLoop, calls=%fused_computation | loop fusion | flops 49152 | bytes 196612 | tf_op jit(solution)/shard_map/jit(_where)/select_n | solution.py:462
  (1 shorter events, 0.0 us)
Async XLA Ops:
  0.6 11.7 %collective-permute-start = (f32[128,128]{1,0:T(8,128)}, f32[128,128]{1,0:T(8,128)S(1)}, u32[]{:S(2)}, u32[]{:S(2)}) collective-permute-start(f32[128,128]{1,0:T(8,128)} %bitcast.6), channel_id=1, source_target_pairs={{3,1},{5,3},{7,5},{9,7},{11,9},{13,11},{15,13},{19,17},{21,19},{23... | collective-permute-start | bytes 196616 | tf_op jit(solution)/shard_map/ppermute | solution.py:437
  1.3 11.0 %collective-permute-start.1 = (f32[128,128]{1,0:T(8,128)}, f32[128,128]{1,0:T(8,128)S(1)}, u32[]{:S(2)}, u32[]{:S(2)}) collective-permute-start(f32[128,128]{1,0:T(8,128)} %bitcast.7), channel_id=1, source_target_pairs={{8,0},{9,1},{10,2},{11,3},{12,4},{13,5},{14,6},{15,7},{0,8},{1,9},... | collective-permute-start | bytes 196616 | tf_op jit(solution)/shard_map/ppermute | solution.py:437
  5.4 6.9 %collective-permute-start.2 = (f32[128,128]{1,0:T(8,128)}, f32[128,128]{1,0:T(8,128)S(1)}, u32[]{:S(2)}, u32[]{:S(2)}) collective-permute-start(f32[128,128]{1,0:T(8,128)} %bitcast.8), channel_id=1, source_target_pairs={{11,1},{13,3},{15,5},{0,10},{2,12},{4,14},{3,9},{5,11},{7,13},{9,1... | collective-permute-start | bytes 196616 | tf_op jit(solution)/shard_map/ppermute | solution.py:437
  18.6 3.0 %collective-permute-start.3 = (f32[64,128]{1,0:T(8,128)S(1)}, f32[64,128]{1,0:T(8,128)S(1)}, u32[]{:S(2)}, u32[]{:S(2)}) collective-permute-start(f32[64,128]{1,0:T(8,128)S(1)} %shard_map.51), channel_id=1, source_target_pairs={{0,1},{1,0},{2,3},{3,2},{4,5},{5,4},{6,7},{7,6},{8,9},{9,8},{10,11... | collective-permute-start | bytes 98312 | tf_op jit(solution)/shard_map/ppermute | solution.py:458
